TPU v7x, 32 devices: a whole 2x2x4 slice. The times are simulated.
32 devices in a mesh: seq: 16 (over z, y, x), head: 2 (over core).
Axes of the slice: x: 2, y: 2, z: 4, core: 2. Of those that a mesh axis runs over, the one named last changes fastest.
Arguments:
- attn_q: bfloat16 [2048, 512], P('seq', 'head'), may hold values from -6 to 6
- attn_k: bfloat16 [2048, 512], P('seq', 'head'), may hold values from -6 to 6
- attn_v: bfloat16 [2048, 512], P('seq', 'head'), may hold values from -6 to 6
- attn_out: bfloat16 [2048, 512], P('seq', 'head'), may hold values from -0.29882812 to 0.29882812
- attn_dout: bfloat16 [2048, 512], P('seq', 'head'), may hold values from -96 to 96
- attn_lse: float32 [4, 2048], P('head', 'seq'), may hold values from 7 to 8
- w_kv: bfloat16 [512, 2, 512], P('seq', None, 'head'), may hold values from -0.25 to 0.25
- gdn_q: bfloat16 [2048, 512], P('seq', 'head'), may hold values from -6 to 6
- gdn_k: bfloat16 [2048, 512], P('seq', 'head'), may hold values from -6 to 6
- gdn_v: bfloat16 [2048, 512], P('seq', 'head'), may hold values from -6 to 6
- gdn_dout: bfloat16 [2048, 512], P('seq', 'head'), may hold values from -6 to 6
- gdn_log_decay: float32 [4, 2048], P('head', 'seq'), may hold values from -0.56 to 0
- gdn_beta: float32 [4, 2048], P('head', 'seq'), may hold values from 0 to 0.9
- gdn_states: float32 [32, 4, 128, 128], P('seq', 'head'), may hold values from -24 to 24
Outputs:
- attn_dq: bfloat16 [2048, 512], P('seq', 'head')
- attn_dx: bfloat16 [512, 2048], P('head', 'seq')
- gdn_dq: bfloat16 [2048, 512], P('seq', 'head')
- gdn_dk: bfloat16 [2048, 512], P('seq', 'head')
- gdn_dv: bfloat16 [2048, 512], P('seq', 'head')
- gdn_dlog_decay: float32 [4, 2048], P('head', 'seq')
- gdn_dbeta: float32 [4, 2048], P('head', 'seq')
All inputs are finite; a program needn't handle non-finite values.
Results may differ from a plain program's by a relative error of at most 0.0078.
Values may be sent and summed in bfloat16 or wider, within the bound.
A program may use at most 64 MiB of HBM per device.

v0:
```python
import jax
import jax.numpy as jnp
from jax import lax
from jax.sharding import PartitionSpec as P

BLOCK = 64
WINDOW = 1024


HIGH = lax.Precision.HIGHEST


def from_behind(block, axis, distance):
    devices = range(lax.axis_size(axis))
    route = [(i - distance, i) for i in devices if i - distance in devices]
    return lax.ppermute(block, axis, route)


def matmul(left_side, right_side):
    return jnp.dot(left_side, right_side, precision=HIGH)


def stack_mul(left_side, right_side):
    return jnp.einsum("hij,hjk->hik", left_side, right_side, precision=HIGH)


def unit_rows(matrix):
    return matrix * lax.rsqrt(jnp.sum(matrix * matrix, axis=-1, keepdims=True) + 1e-06)


def inverse_unit(lower_part):
    length = lower_part.shape[0]
    identity = jnp.eye(length, dtype=jnp.float32)
    powered = lower_part
    result = identity - lower_part
    for _ in range(length.bit_length() - 2):
        powered = matmul(powered, powered)
        result = matmul(result, identity + powered)
    return result


def block_parts(queries, keys_in, decays, strengths):
    length, depth = queries.shape
    unit_q = unit_rows(queries) * depth ** (-0.5)
    unit_k = unit_rows(keys_in)
    summed = jnp.cumsum(decays)
    row_ids = lax.broadcasted_iota(jnp.int32, (length, length), 0)
    col_ids = lax.broadcasted_iota(jnp.int32, (length, length), 1)
    causal = row_ids >= col_ids
    fading = jnp.where(
        causal, jnp.exp(jnp.where(causal, summed[:, None] - summed[None, :], 0.0)), 0.0
    )
    strict = jnp.where(row_ids > col_ids, fading, 0.0)
    lower_part = strengths[:, None] * strict * matmul(unit_k, unit_k.T)
    solved = inverse_unit(lower_part)
    growth = jnp.exp(summed)
    widened = matmul(solved, (strengths * growth)[:, None] * unit_k)
    attention = fading * matmul(unit_q, unit_k.T)
    tailing = jnp.exp(summed[-1] - summed)[:, None] * unit_k
    return (unit_q, solved, growth, widened, attention, tailing)


def block_forward(queries, keys_in, values, decays, strengths, initial):
    unit_q, solved, growth, widened, attention, tailing = block_parts(
        queries, keys_in, decays, strengths
    )
    fresh = matmul(solved, strengths[:, None] * values) - matmul(widened, initial)
    output = growth[:, None] * matmul(unit_q, initial) + matmul(attention, fresh)
    final = growth[-1] * initial + matmul(tailing.T, fresh)
    return (output, final)


def block_adjoint(queries, keys_in, decays, strengths, out_grad):
    unit_q, solved, growth, widened, attention, tailing = block_parts(
        queries, keys_in, decays, strengths
    )
    depth = queries.shape[1]
    carry_map = growth[-1] * jnp.eye(depth, dtype=jnp.float32) - matmul(widened.T, tailing)
    local_term = matmul((growth[:, None] * unit_q).T, out_grad) - matmul(
        widened.T, matmul(attention.T, out_grad)
    )
    return (carry_map, local_term)


def block_grads(queries, keys_in, values, decays, strengths, initial, out_grad, later_adjoint):
    _, pullback = jax.vjp(block_forward, queries, keys_in, values, decays, strengths, initial)
    grad_q, grad_k, grad_v, grad_decay, grad_beta, _ = pullback((out_grad, later_adjoint))
    return (grad_q, grad_k, grad_v, grad_decay, grad_beta)


def window_terms(queries, keys_in, values, out_grad, log_totals, dot_terms, query_pos, key_pos):
    scaling = queries.shape[2] ** (-0.5)
    logits = (
        jnp.einsum("rhd,khd->hrk", queries, keys_in, preferred_element_type=jnp.float32) * scaling
    )
    distance = query_pos[:, None] - key_pos[None, :]
    visible = ((distance >= 0) & (distance < WINDOW) & (key_pos[None, :] >= 0))[None, :, :]
    chances = jnp.where(
        visible, jnp.exp(jnp.where(visible, logits - log_totals[:, :, None], 0.0)), 0.0
    )
    grad_prob = jnp.einsum("rhd,khd->hrk", out_grad, values, preferred_element_type=jnp.float32)
    grad_logit = (chances * (grad_prob - dot_terms[:, :, None])).astype(jnp.bfloat16)
    weights = chances.astype(jnp.bfloat16)
    grad_q = (
        jnp.einsum("hrk,khd->rhd", grad_logit, keys_in, preferred_element_type=jnp.float32)
        * scaling
    )
    grad_k = (
        jnp.einsum("hrk,rhd->khd", grad_logit, queries, preferred_element_type=jnp.float32)
        * scaling
    )
    grad_v = jnp.einsum("hrk,rhd->khd", weights, out_grad, preferred_element_type=jnp.float32)
    return (grad_q, grad_k, grad_v)


def per_device(
    attn_q,
    attn_k,
    attn_v,
    attn_out,
    attn_dout,
    attn_lse,
    w_kv,
    gdn_q,
    gdn_k,
    gdn_v,
    gdn_dout,
    gdn_log_decay,
    gdn_beta,
    gdn_states,
):
    row_count, column_count = attn_q.shape
    head_count = attn_lse.shape[0]
    depth = column_count // head_count
    reach_count = WINDOW // row_count
    position = lax.axis_index("seq")

    def by_heads(matrix):
        return matrix.reshape(-1, head_count, depth)

    dot_terms = jnp.sum(
        by_heads(attn_dout).astype(jnp.float32) * by_heads(attn_out).astype(jnp.float32), axis=2
    ).T
    query_pos = position * row_count + jnp.arange(row_count, dtype=jnp.int32)
    couple = jnp.stack([attn_k, attn_v])
    pieces = []
    for offset_by in range(reach_count, 0, -1):
        pieces.append(from_behind(couple, "seq", offset_by))
    before = jnp.concatenate(pieces, axis=1)
    window = jnp.concatenate([before, couple], axis=1)
    key_pos = (position - reach_count) * row_count + jnp.arange(
        (reach_count + 1) * row_count, dtype=jnp.int32
    )
    grad_q, grad_k, grad_v = window_terms(
        by_heads(attn_q),
        by_heads(window[0]),
        by_heads(window[1]),
        by_heads(attn_dout),
        attn_lse,
        dot_terms,
        query_pos,
        key_pos,
    )
    own_rows = jnp.stack([attn_q, attn_dout])
    own_stats = jnp.stack([attn_lse, dot_terms])
    query_parts = [own_rows]
    stat_parts = [own_stats]
    for offset_by in range(1, reach_count + 1):
        query_parts.append(from_behind(own_rows, "seq", -offset_by))
        stat_parts.append(from_behind(own_stats, "seq", -offset_by))
    later_rows = jnp.concatenate(query_parts, axis=1)
    later_stats = jnp.concatenate(stat_parts, axis=2)
    later_pos = position * row_count + jnp.arange((reach_count + 1) * row_count, dtype=jnp.int32)
    _, own_k, own_v = window_terms(
        by_heads(later_rows[0]),
        by_heads(attn_k),
        by_heads(attn_v),
        by_heads(later_rows[1]),
        later_stats[0],
        later_stats[1],
        later_pos,
        query_pos,
    )
    key_grad = own_k.reshape(row_count, column_count).astype(jnp.bfloat16)
    value_grad = own_v.reshape(row_count, column_count).astype(jnp.bfloat16)
    attn_dq = grad_q.reshape(row_count, column_count).astype(jnp.bfloat16)
    row_piece = lax.all_gather(w_kv, "seq", axis=0, tiled=True)
    from_keys = lax.dot_general(
        row_piece[:, 0, :], key_grad, (((1,), (1,)), ((), ())), preferred_element_type=jnp.float32
    )
    partial_value = from_keys + lax.dot_general(
        row_piece[:, 1, :], value_grad, (((1,), (1,)), ((), ())), preferred_element_type=jnp.float32
    )
    attn_dx = lax.psum_scatter(partial_value, "head", scatter_dimension=0, tiled=True).astype(
        jnp.bfloat16
    )
    block_count = row_count // BLOCK

    def by_blocks(matrix):
        return (
            matrix.reshape(block_count, BLOCK, head_count, depth)
            .transpose(0, 2, 1, 3)
            .astype(jnp.float32)
        )

    def gates_by_blocks(matrix):
        return matrix.reshape(head_count, block_count, BLOCK).transpose(1, 0, 2)

    queries = by_blocks(gdn_q)
    keys_in = by_blocks(gdn_k)
    values = by_blocks(gdn_v)
    out_grad = by_blocks(gdn_dout)
    decays = gates_by_blocks(gdn_log_decay)
    strengths = gates_by_blocks(gdn_beta)
    carry_map, local_term = jax.vmap(jax.vmap(block_adjoint))(
        queries, keys_in, decays, strengths, out_grad
    )
    identity = jnp.broadcast_to(jnp.eye(depth, dtype=jnp.float32), (head_count, depth, depth))
    nothing = jnp.zeros((head_count, depth, depth), jnp.float32)

    def compose_blocks(carry, couple_in):
        across, offset = carry
        return (
            (stack_mul(couple_in[0], across), stack_mul(couple_in[0], offset) + couple_in[1]),
            None,
        )

    (across, offset), _ = lax.scan(
        compose_blocks, (identity, nothing), (carry_map, local_term), reverse=True
    )

    def relay_step(step_no, incoming):
        return from_behind(stack_mul(across, incoming) + offset, "seq", -1)

    carried = lax.fori_loop(0, lax.axis_size("seq") - 1, relay_step, nothing)

    def backward(carry, couple_in):
        return (stack_mul(couple_in[0], carry) + couple_in[1], carry)

    _, later_adjoint = lax.scan(backward, carried, (carry_map, local_term), reverse=True)
    grad_bq, grad_bk, grad_bv, grad_decay, grad_beta = jax.vmap(jax.vmap(block_grads))(
        queries, keys_in, values, decays, strengths, gdn_states, out_grad, later_adjoint
    )

    def tokens_back(stacked):
        return stacked.transpose(0, 2, 1, 3).reshape(row_count, column_count).astype(jnp.bfloat16)

    def per_head(stacked):
        return stacked.transpose(1, 0, 2).reshape(head_count, row_count)

    return (
        attn_dq,
        attn_dx,
        tokens_back(grad_bq),
        tokens_back(grad_bk),
        tokens_back(grad_bv),
        per_head(grad_decay),
        per_head(grad_beta),
    )


def solution(mesh):
    placed = (
        P("seq", "head"),
        P("seq", "head"),
        P("seq", "head"),
        P("seq", "head"),
        P("seq", "head"),
        P("head", "seq"),
        P("seq", None, "head"),
        P("seq", "head"),
        P("seq", "head"),
        P("seq", "head"),
        P("seq", "head"),
        P("head", "seq"),
        P("head", "seq"),
        P("seq", "head", None, None),
    )
    return jax.shard_map(
        per_device,
        mesh=mesh,
        in_specs=placed,
        out_specs=(
            P("seq", "head"),
            P("head", "seq"),
            P("seq", "head"),
            P("seq", "head"),
            P("seq", "head"),
            P("head", "seq"),
            P("head", "seq"),
        ),
        check_vma=False,
    )
```

profile of v0, /device:TPU:0, one launch (start us, length us, event | category | flops | bytes accessed | tf_op | source)
XLA Modules:
  0.0 311.4 jit_solution(4315394593394781818)
XLA Ops:
  25.4 1.3 fusion.50
  30.9 133.4 %while.43 = (s32[]{:T(128)}, f32[2,128,128]{2,1,0:T(8,128)S(1)}, f32[2,128,128]{2,1,0:T(8,128)S(1)}, f32[2,128,128]{2,1,0:T(8,128)S(1)}, s32[]{:T(128)}) while((s32[]{:T(128)}, f32[2,128,128]{2,1,0:T(8,128)S(1)}, f32[2,128,128]{2,1,0:T(8,128)S(1)}, f32[2,128,128]{2,1,0:T(8,128)S(1)}, s32[]{:T(128)}) %tuple.116), condition=%wide.region_9.10_spmd, body=%wide.region_8.9_spmd.sunk | while | flops 50364416 | bytes 1048677 | solution.py:235
  32.5 7.7 %collective-permute-done = f32[2,128,128]{2,1,0:T(8,128)S(1)} collective-permute-done((f32[2,128,128]{2,1,0:T(8,128)S(1)}, f32[2,128,128]{2,1,0:T(8,128)S(1)}, u32[]{:S(2)}, u32[]{:S(2)}) %collective-permute-start) | collective-permute-done | bytes 131104 | tf_op jit(solution)/shard_map/while/body/eval_jaxpr/ppermute | solution.py:16
  41.8 6.8 %collective-permute-done = f32[2,128,128]{2,1,0:T(8,128)S(1)} collective-permute-done((f32[2,128,128]{2,1,0:T(8,128)S(1)}, f32[2,128,128]{2,1,0:T(8,128)S(1)}, u32[]{:S(2)}, u32[]{:S(2)}) %collective-permute-start) | collective-permute-done | bytes 131104 | tf_op jit(solution)/shard_map/while/body/eval_jaxpr/ppermute | solution.py:16
  48.8 1.3 collective-permute-start
  50.1 6.5 %collective-permute-done = f32[2,128,128]{2,1,0:T(8,128)S(1)} collective-permute-done((f32[2,128,128]{2,1,0:T(8,128)S(1)}, f32[2,128,128]{2,1,0:T(8,128)S(1)}, u32[]{:S(2)}, u32[]{:S(2)}) %collective-permute-start) | collective-permute-done | bytes 131104 | tf_op jit(solution)/shard_map/while/body/eval_jaxpr/ppermute | solution.py:16
  58.2 6.5 %collective-permute-done = f32[2,128,128]{2,1,0:T(8,128)S(1)} collective-permute-done((f32[2,128,128]{2,1,0:T(8,128)S(1)}, f32[2,128,128]{2,1,0:T(8,128)S(1)}, u32[]{:S(2)}, u32[]{:S(2)}) %collective-permute-start) | collective-permute-done | bytes 131104 | tf_op jit(solution)/shard_map/while/body/eval_jaxpr/ppermute | solution.py:16
  66.2 6.9 %collective-permute-done = f32[2,128,128]{2,1,0:T(8,128)S(1)} collective-permute-done((f32[2,128,128]{2,1,0:T(8,128)S(1)}, f32[2,128,128]{2,1,0:T(8,128)S(1)}, u32[]{:S(2)}, u32[]{:S(2)}) %collective-permute-start) | collective-permute-done | bytes 131104 | tf_op jit(solution)/shard_map/while/body/eval_jaxpr/ppermute | solution.py:16
  74.7 7.4 %collective-permute-done = f32[2,128,128]{2,1,0:T(8,128)S(1)} collective-permute-done((f32[2,128,128]{2,1,0:T(8,128)S(1)}, f32[2,128,128]{2,1,0:T(8,128)S(1)}, u32[]{:S(2)}, u32[]{:S(2)}) %collective-permute-start) | collective-permute-done | bytes 131104 | tf_op jit(solution)/shard_map/while/body/eval_jaxpr/ppermute | solution.py:16
  83.6 8.7 %collective-permute-done = f32[2,128,128]{2,1,0:T(8,128)S(1)} collective-permute-done((f32[2,128,128]{2,1,0:T(8,128)S(1)}, f32[2,128,128]{2,1,0:T(8,128)S(1)}, u32[]{:S(2)}, u32[]{:S(2)}) %collective-permute-start) | collective-permute-done | bytes 131104 | tf_op jit(solution)/shard_map/while/body/eval_jaxpr/ppermute | solution.py:16
  93.8 8.7 %collective-permute-done = f32[2,128,128]{2,1,0:T(8,128)S(1)} collective-permute-done((f32[2,128,128]{2,1,0:T(8,128)S(1)}, f32[2,128,128]{2,1,0:T(8,128)S(1)}, u32[]{:S(2)}, u32[]{:S(2)}) %collective-permute-start) | collective-permute-done | bytes 131104 | tf_op jit(solution)/shard_map/while/body/eval_jaxpr/ppermute | solution.py:16
  104.2 7.2 %collective-permute-done = f32[2,128,128]{2,1,0:T(8,128)S(1)} collective-permute-done((f32[2,128,128]{2,1,0:T(8,128)S(1)}, f32[2,128,128]{2,1,0:T(8,128)S(1)}, u32[]{:S(2)}, u32[]{:S(2)}) %collective-permute-start) | collective-permute-done | bytes 131104 | tf_op jit(solution)/shard_map/while/body/eval_jaxpr/ppermute | solution.py:16
  112.9 6.8 %collective-permute-done = f32[2,128,128]{2,1,0:T(8,128)S(1)} collective-permute-done((f32[2,128,128]{2,1,0:T(8,128)S(1)}, f32[2,128,128]{2,1,0:T(8,128)S(1)}, u32[]{:S(2)}, u32[]{:S(2)}) %collective-permute-start) | collective-permute-done | bytes 131104 | tf_op jit(solution)/shard_map/while/body/eval_jaxpr/ppermute | solution.py:16
  121.3 7.1 %collective-permute-done = f32[2,128,128]{2,1,0:T(8,128)S(1)} collective-permute-done((f32[2,128,128]{2,1,0:T(8,128)S(1)}, f32[2,128,128]{2,1,0:T(8,128)S(1)}, u32[]{:S(2)}, u32[]{:S(2)}) %collective-permute-start) | collective-permute-done | bytes 131104 | tf_op jit(solution)/shard_map/while/body/eval_jaxpr/ppermute | solution.py:16
  130.0 7.4 %collective-permute-done = f32[2,128,128]{2,1,0:T(8,128)S(1)} collective-permute-done((f32[2,128,128]{2,1,0:T(8,128)S(1)}, f32[2,128,128]{2,1,0:T(8,128)S(1)}, u32[]{:S(2)}, u32[]{:S(2)}) %collective-permute-start) | collective-permute-done | bytes 131104 | tf_op jit(solution)/shard_map/while/body/eval_jaxpr/ppermute | solution.py:16
  138.9 7.4 %collective-permute-done = f32[2,128,128]{2,1,0:T(8,128)S(1)} collective-permute-done((f32[2,128,128]{2,1,0:T(8,128)S(1)}, f32[2,128,128]{2,1,0:T(8,128)S(1)}, u32[]{:S(2)}, u32[]{:S(2)}) %collective-permute-start) | collective-permute-done | bytes 131104 | tf_op jit(solution)/shard_map/while/body/eval_jaxpr/ppermute | solution.py:16
  147.8 7.4 %collective-permute-done = f32[2,128,128]{2,1,0:T(8,128)S(1)} collective-permute-done((f32[2,128,128]{2,1,0:T(8,128)S(1)}, f32[2,128,128]{2,1,0:T(8,128)S(1)}, u32[]{:S(2)}, u32[]{:S(2)}) %collective-permute-start) | collective-permute-done | bytes 131104 | tf_op jit(solution)/shard_map/while/body/eval_jaxpr/ppermute | solution.py:16
  156.8 7.5 %collective-permute-done = f32[2,128,128]{2,1,0:T(8,128)S(1)} collective-permute-done((f32[2,128,128]{2,1,0:T(8,128)S(1)}, f32[2,128,128]{2,1,0:T(8,128)S(1)}, u32[]{:S(2)}, u32[]{:S(2)}) %collective-permute-start) | collective-permute-done | bytes 131104 | tf_op jit(solution)/shard_map/while/body/eval_jaxpr/ppermute | solution.py:16
  164.3 1.5 collective-permute-start.21
  180.5 54.2 %all_gather.3 = bf16[512,2,256]{2,0,1:T(8,128)(2,1)S(1)} all-gather(bf16[32,2,256]{2,0,1:T(8,128)(2,1)S(1)} %copy.284), channel_id=1, replica_groups=mesh['seq'=16,'head'=2] {'seq'}, dimensions={0}, use_global_device_ids=true | all-gather | bytes 557056 | tf_op jit(solution)/shard_map/all_gather | solution.py:187
  236.6 1.4 fusion.41
  242.9 1.3 collective-permute-start.22
  244.3 1.5 collective-permute-start.23
  257.5 1.9 collective-permute-done.11
  260.7 10.6 %collective-permute-start.1 = (bf16[2,128,256]{1,2,0:T(8,128)(2,1)S(1)}, bf16[2,128,256]{1,2,0:T(8,128)(2,1)}, u32[]{:S(2)}, u32[]{:S(2)}) collective-permute-start(bf16[2,128,256]{1,2,0:T(8,128)(2,1)S(1)} %pad_maximum_fusion), channel_id=1, source_target_pairs={{0,16},{2,18},{4,20},{6,22},{8,24},{10,26},{12,28},{14,30},{1,17},... | collective-permute-start | bytes 393224 | tf_op jit(solution)/shard_map/ppermute | solution.py:16
  271.3 6.4 %collective-permute-start.2 = (bf16[2,128,256]{1,2,0:T(8,128)(2,1)S(1)}, bf16[2,128,256]{1,2,0:T(8,128)(2,1)}, u32[]{:S(2)}, u32[]{:S(2)}) collective-permute-start(bf16[2,128,256]{1,2,0:T(8,128)(2,1)S(1)} %pad_maximum_fusion), channel_id=1, source_target_pairs={{0,14},{2,16},{4,18},{6,20},{8,22},{10,24},{12,26},{14,28},{16,30}... | collective-permute-start | bytes 393224 | tf_op jit(solution)/shard_map/ppermute | solution.py:16
  277.7 1.9 collective-permute-start.3
  279.7 2.0 collective-permute-start.4
  281.7 1.9 collective-permute-start.5
  287.8 3.0 collective-permute-start.6
  291.8 1.3 collective-permute-start.7
  294.0 3.1 collective-permute-start.8
  (307 shorter events, 93.0 us)
Async XLA Ops:
  7.2 295.8 %reduce-scatter.2.cloned.1.call-start = ((), (), s32[]{:S(2)}) async-start(), calls=%async_computation.1 | async-start | bytes 393216 | tf_op jit(solution)/shard_map/reduce_scatter | solution.py:194
  10.0 232.9 %collective-permute-start.17 = (f32[2,2,128]{2,1,0:T(2,128)S(1)}, f32[2,2,128]{2,1,0:T(2,128)S(1)}, u32[]{:S(2)}, u32[]{:S(2)}) collective-permute-start(f32[2,2,128]{2,1,0:T(2,128)S(1)} %get-tuple-element.350), channel_id=1, source_target_pairs={{2,0},{4,2},{6,4},{8,6},{10,8},{12,10},{14,12},{16,14},{18,16},{20... | collective-permute-start | bytes 6152 | tf_op jit(solution)/shard_map/ppermute | solution.py:16
  11.3 233.0 %collective-permute-start.18 = (f32[2,2,128]{2,1,0:T(2,128)S(1)}, f32[2,2,128]{2,1,0:T(2,128)S(1)}, u32[]{:S(2)}, u32[]{:S(2)}) collective-permute-start(f32[2,2,128]{2,1,0:T(2,128)S(1)} %get-tuple-element.350), channel_id=1, source_target_pairs={{4,0},{6,2},{8,4},{10,6},{12,8},{14,10},{16,12},{18,14},{20,16},{2... | collective-permute-start | bytes 6152 | tf_op jit(solution)/shard_map/ppermute | solution.py:16
  12.6 233.2 %collective-permute-start.19 = (f32[2,2,128]{2,1,0:T(2,128)S(1)}, f32[2,2,128]{2,1,0:T(2,128)S(1)}, u32[]{:S(2)}, u32[]{:S(2)}) collective-permute-start(f32[2,2,128]{2,1,0:T(2,128)S(1)} %get-tuple-element.350), channel_id=1, source_target_pairs={{6,0},{8,2},{10,4},{12,6},{14,8},{16,10},{18,12},{20,14},{22,16},{... | collective-permute-start | bytes 6152 | tf_op jit(solution)/shard_map/ppermute | solution.py:16
  13.9 233.2 %collective-permute-start.20 = (f32[2,2,128]{2,1,0:T(2,128)S(1)}, f32[2,2,128]{2,1,0:T(2,128)S(1)}, u32[]{:S(2)}, u32[]{:S(2)}) collective-permute-start(f32[2,2,128]{2,1,0:T(2,128)S(1)} %get-tuple-element.350), channel_id=1, source_target_pairs={{8,0},{10,2},{12,4},{14,6},{16,8},{18,10},{20,12},{22,14},{24,16},... | collective-permute-start | bytes 6152 | tf_op jit(solution)/shard_map/ppermute | solution.py:16
  31.2 9.0 %collective-permute-start = (f32[2,128,128]{2,1,0:T(8,128)S(1)}, f32[2,128,128]{2,1,0:T(8,128)S(1)}, u32[]{:S(2)}, u32[]{:S(2)}) collective-permute-start(f32[2,128,128]{2,1,0:T(8,128)S(1)} %convolution_add_fusion.20), channel_id=1, source_target_pairs={{2,0},{4,2},{6,4},{8,6},{10,8},{12,10},{14,12},{16,14},{18,16},{20... | collective-permute-start | bytes 393224 | tf_op jit(solution)/shard_map/while/body/eval_jaxpr/ppermute | solution.py:16
  40.4 8.1 %collective-permute-start = (f32[2,128,128]{2,1,0:T(8,128)S(1)}, f32[2,128,128]{2,1,0:T(8,128)S(1)}, u32[]{:S(2)}, u32[]{:S(2)}) collective-permute-start(f32[2,128,128]{2,1,0:T(8,128)S(1)} %convolution_add_fusion.20), channel_id=1, source_target_pairs={{2,0},{4,2},{6,4},{8,6},{10,8},{12,10},{14,12},{16,14},{18,16},{20... | collective-permute-start | bytes 393224 | tf_op jit(solution)/shard_map/while/body/eval_jaxpr/ppermute | solution.py:16
  64.9 8.2 %collective-permute-start = (f32[2,128,128]{2,1,0:T(8,128)S(1)}, f32[2,128,128]{2,1,0:T(8,128)S(1)}, u32[]{:S(2)}, u32[]{:S(2)}) collective-permute-start(f32[2,128,128]{2,1,0:T(8,128)S(1)} %convolution_add_fusion.20), channel_id=1, source_target_pairs={{2,0},{4,2},{6,4},{8,6},{10,8},{12,10},{14,12},{16,14},{18,16},{20... | collective-permute-start | bytes 393224 | tf_op jit(solution)/shard_map/while/body/eval_jaxpr/ppermute | solution.py:16
  73.4 8.7 %collective-permute-start = (f32[2,128,128]{2,1,0:T(8,128)S(1)}, f32[2,128,128]{2,1,0:T(8,128)S(1)}, u32[]{:S(2)}, u32[]{:S(2)}) collective-permute-start(f32[2,128,128]{2,1,0:T(8,128)S(1)} %convolution_add_fusion.20), channel_id=1, source_target_pairs={{2,0},{4,2},{6,4},{8,6},{10,8},{12,10},{14,12},{16,14},{18,16},{20... | collective-permute-start | bytes 393224 | tf_op jit(solution)/shard_map/while/body/eval_jaxpr/ppermute | solution.py:16
  82.3 10.0 %collective-permute-start = (f32[2,128,128]{2,1,0:T(8,128)S(1)}, f32[2,128,128]{2,1,0:T(8,128)S(1)}, u32[]{:S(2)}, u32[]{:S(2)}) collective-permute-start(f32[2,128,128]{2,1,0:T(8,128)S(1)} %convolution_add_fusion.20), channel_id=1, source_target_pairs={{2,0},{4,2},{6,4},{8,6},{10,8},{12,10},{14,12},{16,14},{18,16},{20... | collective-permute-start | bytes 393224 | tf_op jit(solution)/shard_map/while/body/eval_jaxpr/ppermute | solution.py:16
  92.5 10.0 %collective-permute-start = (f32[2,128,128]{2,1,0:T(8,128)S(1)}, f32[2,128,128]{2,1,0:T(8,128)S(1)}, u32[]{:S(2)}, u32[]{:S(2)}) collective-permute-start(f32[2,128,128]{2,1,0:T(8,128)S(1)} %convolution_add_fusion.20), channel_id=1, source_target_pairs={{2,0},{4,2},{6,4},{8,6},{10,8},{12,10},{14,12},{16,14},{18,16},{20... | collective-permute-start | bytes 393224 | tf_op jit(solution)/shard_map/while/body/eval_jaxpr/ppermute | solution.py:16
  102.9 8.5 %collective-permute-start = (f32[2,128,128]{2,1,0:T(8,128)S(1)}, f32[2,128,128]{2,1,0:T(8,128)S(1)}, u32[]{:S(2)}, u32[]{:S(2)}) collective-permute-start(f32[2,128,128]{2,1,0:T(8,128)S(1)} %convolution_add_fusion.20), channel_id=1, source_target_pairs={{2,0},{4,2},{6,4},{8,6},{10,8},{12,10},{14,12},{16,14},{18,16},{20... | collective-permute-start | bytes 393224 | tf_op jit(solution)/shard_map/while/body/eval_jaxpr/ppermute | solution.py:16
  111.6 8.1 %collective-permute-start = (f32[2,128,128]{2,1,0:T(8,128)S(1)}, f32[2,128,128]{2,1,0:T(8,128)S(1)}, u32[]{:S(2)}, u32[]{:S(2)}) collective-permute-start(f32[2,128,128]{2,1,0:T(8,128)S(1)} %convolution_add_fusion.20), channel_id=1, source_target_pairs={{2,0},{4,2},{6,4},{8,6},{10,8},{12,10},{14,12},{16,14},{18,16},{20... | collective-permute-start | bytes 393224 | tf_op jit(solution)/shard_map/while/body/eval_jaxpr/ppermute | solution.py:16
  120.0 8.4 %collective-permute-start = (f32[2,128,128]{2,1,0:T(8,128)S(1)}, f32[2,128,128]{2,1,0:T(8,128)S(1)}, u32[]{:S(2)}, u32[]{:S(2)}) collective-permute-start(f32[2,128,128]{2,1,0:T(8,128)S(1)} %convolution_add_fusion.20), channel_id=1, source_target_pairs={{2,0},{4,2},{6,4},{8,6},{10,8},{12,10},{14,12},{16,14},{18,16},{20... | collective-permute-start | bytes 393224 | tf_op jit(solution)/shard_map/while/body/eval_jaxpr/ppermute | solution.py:16
  128.7 8.7 %collective-permute-start = (f32[2,128,128]{2,1,0:T(8,128)S(1)}, f32[2,128,128]{2,1,0:T(8,128)S(1)}, u32[]{:S(2)}, u32[]{:S(2)}) collective-permute-start(f32[2,128,128]{2,1,0:T(8,128)S(1)} %convolution_add_fusion.20), channel_id=1, source_target_pairs={{2,0},{4,2},{6,4},{8,6},{10,8},{12,10},{14,12},{16,14},{18,16},{20... | collective-permute-start | bytes 393224 | tf_op jit(solution)/shard_map/while/body/eval_jaxpr/ppermute | solution.py:16
  137.6 8.7 %collective-permute-start = (f32[2,128,128]{2,1,0:T(8,128)S(1)}, f32[2,128,128]{2,1,0:T(8,128)S(1)}, u32[]{:S(2)}, u32[]{:S(2)}) collective-permute-start(f32[2,128,128]{2,1,0:T(8,128)S(1)} %convolution_add_fusion.20), channel_id=1, source_target_pairs={{2,0},{4,2},{6,4},{8,6},{10,8},{12,10},{14,12},{16,14},{18,16},{20... | collective-permute-start | bytes 393224 | tf_op jit(solution)/shard_map/while/body/eval_jaxpr/ppermute | solution.py:16
  146.5 8.7 %collective-permute-start = (f32[2,128,128]{2,1,0:T(8,128)S(1)}, f32[2,128,128]{2,1,0:T(8,128)S(1)}, u32[]{:S(2)}, u32[]{:S(2)}) collective-permute-start(f32[2,128,128]{2,1,0:T(8,128)S(1)} %convolution_add_fusion.20), channel_id=1, source_target_pairs={{2,0},{4,2},{6,4},{8,6},{10,8},{12,10},{14,12},{16,14},{18,16},{20... | collective-permute-start | bytes 393224 | tf_op jit(solution)/shard_map/while/body/eval_jaxpr/ppermute | solution.py:16
  155.5 8.8 %collective-permute-start = (f32[2,128,128]{2,1,0:T(8,128)S(1)}, f32[2,128,128]{2,1,0:T(8,128)S(1)}, u32[]{:S(2)}, u32[]{:S(2)}) collective-permute-start(f32[2,128,128]{2,1,0:T(8,128)S(1)} %convolution_add_fusion.20), channel_id=1, source_target_pairs={{2,0},{4,2},{6,4},{8,6},{10,8},{12,10},{14,12},{16,14},{18,16},{20... | collective-permute-start | bytes 393224 | tf_op jit(solution)/shard_map/while/body/eval_jaxpr/ppermute | solution.py:16
  164.3 84.2 %collective-permute-start.21 = (f32[2,2,128]{2,1,0:T(2,128)S(1)}, f32[2,2,128]{2,1,0:T(2,128)S(1)}, u32[]{:S(2)}, u32[]{:S(2)}) collective-permute-start(f32[2,2,128]{2,1,0:T(2,128)S(1)} %get-tuple-element.350), channel_id=1, source_target_pairs={{10,0},{12,2},{14,4},{16,6},{18,8},{20,10},{22,12},{24,14},{26,16}... | collective-permute-start | bytes 6152 | tf_op jit(solution)/shard_map/ppermute | solution.py:16
  249.8 9.6 %collective-permute-start.11 = (bf16[2,128,256]{1,2,0:T(8,128)(2,1)S(1)}, bf16[2,128,256]{1,2,0:T(8,128)(2,1)S(1)}, u32[]{:S(2)}, u32[]{:S(2)}) collective-permute-start(bf16[2,128,256]{1,2,0:T(8,128)(2,1)S(1)} %get-tuple-element.334), channel_id=1, source_target_pairs={{6,0},{8,2},{10,4},{12,6},{14,8},{16,10},{18,12},{20,14},{22,16},{... | collective-permute-start | bytes 393224 | tf_op jit(solution)/shard_map/ppermute | solution.py:16
  251.5 9.1 %collective-permute-start.12 = (bf16[2,128,256]{1,2,0:T(8,128)(2,1)S(1)}, bf16[2,128,256]{1,2,0:T(8,128)(2,1)S(1)}, u32[]{:S(2)}, u32[]{:S(2)}) collective-permute-start(bf16[2,128,256]{1,2,0:T(8,128)(2,1)S(1)} %get-tuple-element.334), channel_id=1, source_target_pairs={{8,0},{10,2},{12,4},{14,6},{16,8},{18,10},{20,12},{22,14},{24,16},... | collective-permute-start | bytes 393224 | tf_op jit(solution)/shard_map/ppermute | solution.py:16
  252.8 18.4 %collective-permute-start.13 = (bf16[2,128,256]{1,2,0:T(8,128)(2,1)S(1)}, bf16[2,128,256]{1,2,0:T(8,128)(2,1)S(1)}, u32[]{:S(2)}, u32[]{:S(2)}) collective-permute-start(bf16[2,128,256]{1,2,0:T(8,128)(2,1)S(1)} %get-tuple-element.334), channel_id=1, source_target_pairs={{10,0},{12,2},{14,4},{16,6},{18,8},{20,10},{22,12},{24,14},{26,16}... | collective-permute-start | bytes 393224 | tf_op jit(solution)/shard_map/ppermute | solution.py:16
  254.8 22.9 %collective-permute-start.14 = (bf16[2,128,256]{1,2,0:T(8,128)(2,1)S(1)}, bf16[2,128,256]{1,2,0:T(8,128)(2,1)S(1)}, u32[]{:S(2)}, u32[]{:S(2)}) collective-permute-start(bf16[2,128,256]{1,2,0:T(8,128)(2,1)S(1)} %get-tuple-element.334), channel_id=1, source_target_pairs={{12,0},{14,2},{16,4},{18,6},{20,8},{22,10},{24,12},{26,14},{28,16}... | collective-permute-start | bytes 393224 | tf_op jit(solution)/shard_map/ppermute | solution.py:16
  256.1 23.6 %collective-permute-start.15 = (bf16[2,128,256]{1,2,0:T(8,128)(2,1)S(1)}, bf16[2,128,256]{1,2,0:T(8,128)(2,1)S(1)}, u32[]{:S(2)}, u32[]{:S(2)}) collective-permute-start(bf16[2,128,256]{1,2,0:T(8,128)(2,1)S(1)} %get-tuple-element.334), channel_id=1, source_target_pairs={{14,0},{16,2},{18,4},{20,6},{22,8},{24,10},{26,12},{28,14},{30,16}... | collective-permute-start | bytes 393224 | tf_op jit(solution)/shard_map/ppermute | solution.py:16
  259.3 22.4 %collective-permute-start.16 = (bf16[2,128,256]{1,2,0:T(8,128)(2,1)S(1)}, bf16[2,128,256]{1,2,0:T(8,128)(2,1)S(1)}, u32[]{:S(2)}, u32[]{:S(2)}) collective-permute-start(bf16[2,128,256]{1,2,0:T(8,128)(2,1)S(1)} %get-tuple-element.334), channel_id=1, source_target_pairs={{16,0},{18,2},{20,4},{22,6},{24,8},{26,10},{28,12},{30,14},{17,1},... | collective-permute-start | bytes 393224 | tf_op jit(solution)/shard_map/ppermute | solution.py:16
  260.7 27.2 %collective-permute-start.1 = (bf16[2,128,256]{1,2,0:T(8,128)(2,1)S(1)}, bf16[2,128,256]{1,2,0:T(8,128)(2,1)}, u32[]{:S(2)}, u32[]{:S(2)}) collective-permute-start(bf16[2,128,256]{1,2,0:T(8,128)(2,1)S(1)} %pad_maximum_fusion), channel_id=1, source_target_pairs={{0,16},{2,18},{4,20},{6,22},{8,24},{10,26},{12,28},{14,30},{1,17},... | collective-permute-start | bytes 393224 | tf_op jit(solution)/shard_map/ppermute | solution.py:16
  271.3 20.5 %collective-permute-start.2 = (bf16[2,128,256]{1,2,0:T(8,128)(2,1)S(1)}, bf16[2,128,256]{1,2,0:T(8,128)(2,1)}, u32[]{:S(2)}, u32[]{:S(2)}) collective-permute-start(bf16[2,128,256]{1,2,0:T(8,128)(2,1)S(1)} %pad_maximum_fusion), channel_id=1, source_target_pairs={{0,14},{2,16},{4,18},{6,20},{8,22},{10,24},{12,26},{14,28},{16,30}... | collective-permute-start | bytes 393224 | tf_op jit(solution)/shard_map/ppermute | solution.py:16
  277.7 16.3 %collective-permute-start.3 = (bf16[2,128,256]{1,2,0:T(8,128)(2,1)S(1)}, bf16[2,128,256]{1,2,0:T(8,128)(2,1)}, u32[]{:S(2)}, u32[]{:S(2)}) collective-permute-start(bf16[2,128,256]{1,2,0:T(8,128)(2,1)S(1)} %pad_maximum_fusion), channel_id=1, source_target_pairs={{0,12},{2,14},{4,16},{6,18},{8,20},{10,22},{12,24},{14,26},{16,28}... | collective-permute-start | bytes 393224 | tf_op jit(solution)/shard_map/ppermute | solution.py:16
  279.7 18.4 %collective-permute-start.4 = (bf16[2,128,256]{1,2,0:T(8,128)(2,1)S(1)}, bf16[2,128,256]{1,2,0:T(8,128)(2,1)}, u32[]{:S(2)}, u32[]{:S(2)}) collective-permute-start(bf16[2,128,256]{1,2,0:T(8,128)(2,1)S(1)} %pad_maximum_fusion), channel_id=1, source_target_pairs={{0,10},{2,12},{4,14},{6,16},{8,18},{10,20},{12,22},{14,24},{16,26}... | collective-permute-start | bytes 393224 | tf_op jit(solution)/shard_map/ppermute | solution.py:16
  281.7 17.3 %collective-permute-start.5 = (bf16[2,128,256]{1,2,0:T(8,128)(2,1)S(1)}, bf16[2,128,256]{1,2,0:T(8,128)(2,1)}, u32[]{:S(2)}, u32[]{:S(2)}) collective-permute-start(bf16[2,128,256]{1,2,0:T(8,128)(2,1)S(1)} %pad_maximum_fusion), channel_id=1, source_target_pairs={{0,8},{2,10},{4,12},{6,14},{8,16},{10,18},{12,20},{14,22},{16,24},... | collective-permute-start | bytes 393224 | tf_op jit(solution)/shard_map/ppermute | solution.py:16
  287.8 12.1 %collective-permute-start.6 = (bf16[2,128,256]{1,2,0:T(8,128)(2,1)S(1)}, bf16[2,128,256]{1,2,0:T(8,128)(2,1)S(1)}, u32[]{:S(2)}, u32[]{:S(2)}) collective-permute-start(bf16[2,128,256]{1,2,0:T(8,128)(2,1)S(1)} %pad_maximum_fusion), channel_id=1, source_target_pairs={{0,6},{2,8},{4,10},{6,12},{8,14},{10,16},{12,18},{14,20},{16,22},{... | collective-permute-start | bytes 393224 | tf_op jit(solution)/shard_map/ppermute | solution.py:16
  291.8 8.3 %collective-permute-start.7 = (bf16[2,128,256]{1,2,0:T(8,128)(2,1)S(1)}, bf16[2,128,256]{1,2,0:T(8,128)(2,1)S(1)}, u32[]{:S(2)}, u32[]{:S(2)}) collective-permute-start(bf16[2,128,256]{1,2,0:T(8,128)(2,1)S(1)} %pad_maximum_fusion), channel_id=1, source_target_pairs={{0,4},{2,6},{4,8},{6,10},{8,12},{10,14},{12,16},{14,18},{16,20},{1... | collective-permute-start | bytes 393224 | tf_op jit(solution)/shard_map/ppermute | solution.py:16
  (41 other events, 303.9 us)
Sparse Core Ops, SparseCore 0:
  288.0 4.5 reduce-scatter.1
where the time goes:
time: 313 us; the launch traced here: 311 us
  waiting for transfers between devices  112 us (36%)
  starting transfers between devices  70.6 us (23%)
  blocking collectives  54.2 us (17%)
  matrix products  31.3 us (10%)
  local copies, waits for them, and re-layouts  19.6 us (6%)
  between operations  15.6 us (5%)
  other arithmetic  7.44 us (2%)
    ppermute x39, waiting for transfers between devices, from_behind(): return lax.ppermute(block, axis, route)  112 us
    ppermute x39, starting transfers between devices, from_behind(): return lax.ppermute(block, axis, route)  70.6 us
    all_gather x1, blocking collectives, per_device(): row_piece = lax.all_gather(w_kv, 'seq', axis=0, tiled=True)  54.2 us
    dot_general x53, matrix products, matmul(): return jnp.dot(left_side, right_side, precision=HIGH)  21.9 us
    unnamed x98, local copies, waits for them, and re-layouts  11.8 us
  transfers between devices with their start and end apart: 40, of which 17 were waited for; matrix products, arithmetic and copies ran while one was open for 16% of the time, Pallas kernels for 0%

commit v1 on v0

v1 whole, which is shorter than its diff:
```python
import functools
import jax
import jax.numpy as jnp
from jax import lax
from jax.experimental import pallas as pl
from jax.experimental.pallas import tpu as pltpu
from jax.sharding import PartitionSpec as P

BLOCK = 64
WINDOW = 1024
EPS = 1e-06
MESH = pl.DeviceIdType.MESH
F32 = jnp.float32
BF16 = jnp.bfloat16

NN = (((1,), (0,)), ((), ()))
NT = (((1,), (1,)), ((), ()))
TN = (((0,), (0,)), ((), ()))


def dot(left, right, dims=NN):
    return lax.dot_general(left, right, dims, preferred_element_type=F32)


def split(matrix):
    high = matrix.astype(BF16)
    return high, (matrix - high.astype(F32)).astype(BF16)


def mm(left, right, dims=NN):
    left_high, left_low = split(left)
    right_high, right_low = split(right)
    return dot(left_high, right_high, dims) + (
        dot(left_high, right_low, dims) + dot(left_low, right_high, dims)
    )


def mm_full(left, right, dims=NN):
    return lax.dot_general(
        left, right, dims, precision=lax.Precision.HIGHEST, preferred_element_type=F32
    )


def row_sum(matrix):
    return jnp.sum(matrix, axis=1, keepdims=True)


def column_sum(matrix):
    return jnp.sum(matrix, axis=0, keepdims=True)


def stack_heads(matrix, heads):
    depth = matrix.shape[1] // heads
    return jnp.concatenate([matrix[:, h * depth : (h + 1) * depth] for h in range(heads)], axis=0)


def group_size(count):
    size = 1
    while size * size < count:
        size *= 2
    return size if count % size == 0 else count


def kernel(
    n,
    head_n,
    q_ref, k_ref, v_ref, out_ref, dout_ref, lse_ref, w_ref,
    gq_ref, gk_ref, gv_ref, gdo_ref, decay_ref, beta_ref, states_ref,
    dq_out, dx_out, gdq_out, gdk_out, gdv_out, gdecay_out, gbeta_out,
    kv_buf, qd_buf, stat_own, stat_buf, w_all, ab_buf, carry_in, carry_out, dx_send, dx_recv,
    dq_acc, dkv_acc, map_buf,
    kv_send, kv_recv, qd_send, qd_recv, st_send, st_recv, w_send, w_recv,
    ab_send, ab_recv, c_send, c_recv, x_send, x_recv,
):
    me = lax.axis_index("seq")
    my_head = lax.axis_index("head")
    rows, columns = q_ref.shape
    heads = lse_ref.shape[0]
    depth = columns // heads
    reach = WINDOW // rows
    blocks = rows // BLOCK
    total = heads * rows
    size = group_size(n)
    groups = n // size
    rank = lax.rem(me, size)
    group = lax.div(me, size)
    first = group * size

    barrier = pltpu.get_barrier_semaphore()
    for j in range(1, n):
        pl.semaphore_signal(
            barrier, inc=1, device_id={"seq": lax.rem(me + j, n)}, device_id_type=MESH
        )
    for j in range(1, head_n):
        pl.semaphore_signal(
            barrier, inc=1, device_id={"head": lax.rem(my_head + j, head_n)}, device_id_type=MESH
        )

    ones = jnp.ones((8, depth), F32)
    for h in range(heads):
        cols = slice(h * depth, (h + 1) * depth)
        product = dout_ref[:, cols].astype(F32) * out_ref[:, cols].astype(F32)
        stat_own[h : h + 1, :] = lse_ref[h : h + 1, :]
        stat_own[heads + h : heads + h + 1, :] = mm_full(ones, product, NT)[0:1, :]
    pl.semaphore_wait(barrier, n - 1 + head_n - 1)

    def kv_copy(j, which):
        return pltpu.make_async_remote_copy(
            src_ref=(k_ref, v_ref)[which],
            dst_ref=kv_buf.at[j - 1, which],
            send_sem=kv_send.at[j - 1, which],
            recv_sem=kv_recv.at[j - 1, which],
            device_id={"seq": lax.rem(me + j, n)},
            device_id_type=MESH,
        )

    def qd_copy(j, which):
        return pltpu.make_async_remote_copy(
            src_ref=(q_ref, dout_ref)[which],
            dst_ref=qd_buf.at[j - 1, which],
            send_sem=qd_send.at[j - 1, which],
            recv_sem=qd_recv.at[j - 1, which],
            device_id={"seq": lax.rem(me + n - j, n)},
            device_id_type=MESH,
        )

    def st_copy(j):
        return pltpu.make_async_remote_copy(
            src_ref=stat_own,
            dst_ref=stat_buf.at[j - 1],
            send_sem=st_send.at[j - 1],
            recv_sem=st_recv.at[j - 1],
            device_id={"seq": lax.rem(me + n - j, n)},
            device_id_type=MESH,
        )

    w_rows = w_ref.shape[0]

    def w_copy(j):
        return pltpu.make_async_remote_copy(
            src_ref=w_ref,
            dst_ref=w_all.at[me],
            send_sem=w_send.at[j - 1],
            recv_sem=w_recv.at[j - 1],
            device_id={"seq": lax.rem(me + j, n)},
            device_id_type=MESH,
        )

    def ab_copy(j):
        return pltpu.make_async_remote_copy(
            src_ref=ab_buf.at[rank],
            dst_ref=ab_buf.at[rank],
            send_sem=ab_send.at[j - 1],
            recv_sem=ab_recv.at[j - 1],
            device_id={"seq": first + lax.rem(rank + j, size)},
            device_id_type=MESH,
        )

    def carry_copy():
        return pltpu.make_async_remote_copy(
            src_ref=carry_out,
            dst_ref=carry_in,
            send_sem=c_send,
            recv_sem=c_recv,
            device_id={"seq": lax.rem(me + n - size, n)},
            device_id_type=MESH,
        )

    last_reach = min(reach, n - 1)
    near = min(size, last_reach)

    def start_offsets(low, high):
        for j in range(low, high + 1):
            @pl.when(me + j < n)
            def _():
                kv_copy(j, 0).start()
                kv_copy(j, 1).start()

            @pl.when(me - j >= 0)
            def _():
                qd_copy(j, 0).start()
                qd_copy(j, 1).start()
                st_copy(j).start()

    start_offsets(1, near)

    row_ids = lax.broadcasted_iota(jnp.int32, (total, total), 0)
    col_ids = lax.broadcasted_iota(jnp.int32, (total, total), 1)
    shift = BLOCK.bit_length() - 1
    same = lax.shift_right_logical(row_ids, shift) == lax.shift_right_logical(col_ids, shift)
    eye = row_ids == col_ids
    causal = same & (row_ids >= col_ids)
    strict = same & (row_ids > col_ids)

    def to_column(row):
        return row_sum(jnp.where(eye, row, 0.0))

    def to_row(column):
        return column_sum(jnp.where(eye, column, 0.0))

    def flat_row(ref):
        return jnp.concatenate([ref[h : h + 1, :] for h in range(heads)], axis=1)

    decay_row = flat_row(decay_ref)
    decay_col = to_column(decay_row)
    beta = to_column(flat_row(beta_ref))
    summed = row_sum(jnp.where(causal, decay_row, 0.0))
    summed_row = column_sum(jnp.where(same & (row_ids <= col_ids), decay_col, 0.0))
    whole = row_sum(jnp.where(same, decay_row, 0.0))
    growth = jnp.exp(summed)
    tail = jnp.exp(row_sum(jnp.where(same & (row_ids < col_ids), decay_row, 0.0)))
    end_growth = jnp.exp(whole)
    raw_q = stack_heads(gq_ref[...], heads).astype(F32)
    raw_k = stack_heads(gk_ref[...], heads).astype(F32)
    values = stack_heads(gv_ref[...], heads).astype(F32)
    out_grad = stack_heads(gdo_ref[...], heads).astype(F32)
    inv_q = lax.rsqrt(row_sum(raw_q * raw_q) + EPS)
    inv_k = lax.rsqrt(row_sum(raw_k * raw_k) + EPS)
    scaling = depth ** (-0.5)
    unit_q = raw_q * inv_q * scaling
    unit_k = raw_k * inv_k
    fading = jnp.where(causal, jnp.exp(jnp.where(causal, summed - summed_row, 0.0)), 0.0)
    products = mm(jnp.concatenate([unit_k, unit_q], axis=0), unit_k, NT)
    key_products = products[:total]
    query_products = products[total:]
    strict_fading = jnp.where(strict, fading, 0.0)
    faded_keys = strict_fading * key_products
    lower = beta * faded_keys
    solved = jnp.where(eye, 1.0, 0.0) - lower
    powered = mm_full(lower, lower)
    for step in range(BLOCK.bit_length() - 2):
        if step < BLOCK.bit_length() - 3:
            both = mm_full(jnp.concatenate([solved, powered], axis=0), powered)
            solved = solved + both[:total]
            powered = both[total:]
        else:
            solved = solved + mm_full(solved, powered)
    attention = fading * query_products
    widened = mm(solved, (beta * growth) * unit_k)
    pulled = mm(attention, out_grad, TN)
    tailing = tail * unit_k
    grown_q = growth * unit_q

    def part(matrix, h, b):
        start = h * rows + b * BLOCK
        return matrix[start : start + BLOCK]

    depth_eye = jnp.where(
        lax.broadcasted_iota(jnp.int32, (depth, depth), 0)
        == lax.broadcasted_iota(jnp.int32, (depth, depth), 1),
        1.0,
        0.0,
    )
    for h in range(heads):
        across = None
        for b in reversed(range(blocks)):
            wide = part(widened, h, b)
            right = jnp.concatenate([part(tailing, h, b), part(pulled, h, b)], axis=1)
            product = mm(wide, right, TN)
            carry_map = part(end_growth, h, b)[0:1, :] * depth_eye - product[:, :depth]
            local = mm(part(grown_q, h, b), part(out_grad, h, b), TN) - product[:, depth:]
            map_buf[h, b, :, :depth] = carry_map
            map_buf[h, b, :, depth:] = local
            if across is None:
                across, offset = carry_map, local
            else:
                joined = mm(carry_map, jnp.concatenate([across, offset], axis=1))
                across, offset = joined[:, :depth], joined[:, depth:] + local
        ab_buf[rank, h, :, :depth] = (across - depth_eye).astype(BF16)
        ab_buf[rank, h, :, depth:] = offset.astype(BF16)

    key_ids = lax.broadcasted_iota(jnp.int32, (rows, rows), 0)
    query_ids = lax.broadcasted_iota(jnp.int32, (rows, rows), 1)

    def pair_terms(keys, vals, queries, grads, lse, dots, mask):
        logits = dot(keys, queries, NT) * scaling
        shifted = logits - lse
        if mask is None:
            chances = jnp.exp(shifted)
        else:
            chances = jnp.where(mask, jnp.exp(jnp.where(mask, shifted, 0.0)), 0.0)
        grad_prob = dot(vals, grads, NT)
        return (chances * (grad_prob - dots)).astype(BF16), chances.astype(BF16)

    def cut(ref_value, h):
        return ref_value[:, h * depth : (h + 1) * depth]

    for h in range(heads):
        grad_logit, weights = pair_terms(
            cut(k_ref, h), cut(v_ref, h), cut(q_ref, h), cut(dout_ref, h),
            stat_own[h : h + 1, :], stat_own[heads + h : heads + h + 1, :], query_ids >= key_ids,
        )
        cols = slice(h * depth, (h + 1) * depth)
        dq_acc[:, cols] = dot(grad_logit, cut(k_ref, h), TN)
        dkv_acc[:, cols] = dot(grad_logit, cut(q_ref, h))
        dkv_acc[:, columns + h * depth : columns + (h + 1) * depth] = dot(weights, cut(dout_ref, h))

    for j in range(1, size):
        ab_copy(j).start()
    start_offsets(near + 1, last_reach)
    for j in range(1, n):
        w_copy(j).start()

    def attend(low, high):
        for j in range(low, high + 1):
            mask = query_ids + j * rows - key_ids < WINDOW if (j + 1) * rows > WINDOW else None

            @pl.when(me - j >= 0)
            def _():
                kv_copy(j, 0).wait_recv()
                kv_copy(j, 1).wait_recv()
                for h in range(heads):
                    cols = slice(h * depth, (h + 1) * depth)
                    keys = kv_buf[j - 1, 0, :, cols]
                    grad_logit, _ = pair_terms(
                        keys, kv_buf[j - 1, 1, :, cols], cut(q_ref, h), cut(dout_ref, h),
                        stat_own[h : h + 1, :], stat_own[heads + h : heads + h + 1, :], mask,
                    )
                    dq_acc[:, cols] += dot(grad_logit, keys, TN)

            @pl.when(me + j < n)
            def _():
                qd_copy(j, 0).wait_recv()
                qd_copy(j, 1).wait_recv()
                st_copy(j).wait_recv()
                for h in range(heads):
                    cols = slice(h * depth, (h + 1) * depth)
                    queries = qd_buf[j - 1, 0, :, cols]
                    grads = qd_buf[j - 1, 1, :, cols]
                    grad_logit, weights = pair_terms(
                        cut(k_ref, h), cut(v_ref, h), queries, grads,
                        stat_buf[j - 1, h : h + 1, :],
                        stat_buf[j - 1, heads + h : heads + h + 1, :], mask,
                    )
                    dkv_acc[:, cols] += dot(grad_logit, queries)
                    dkv_acc[:, columns + h * depth : columns + (h + 1) * depth] += dot(
                        weights, grads
                    )

    for j in range(1, size):
        ab_copy(j).wait_recv()
    inside = []
    for h in range(heads):
        joined = jnp.concatenate([depth_eye, jnp.zeros((depth, depth), F32)], axis=1)
        suffix = joined
        for r in reversed(range(size)):
            suffix = jnp.where(rank == r, joined, suffix)
            change = ab_buf[r, h, :, :depth]
            later = joined
            high, low = split(later)
            joined = later + (dot(change, high) + dot(change, low))
            joined = jnp.concatenate(
                [joined[:, :depth], joined[:, depth:] + ab_buf[r, h, :, depth:].astype(F32)], axis=1
            )
        inside.append((joined, suffix))

    @pl.when(group == groups - 1)
    def _():
        carry_in[...] = jnp.zeros_like(carry_in)

    if groups > 1:
        @pl.when(group < groups - 1)
        def _():
            carry_copy().wait_recv()

    for h in range(heads):
        joined, _ = inside[h]
        high, low = split(joined[:, :depth])
        state = carry_in[h]
        carry_out[h] = (dot(high, state) + dot(low, state) + joined[:, depth:]).astype(BF16)
    if groups > 1:
        @pl.when(group > 0)
        def _():
            carry_copy().start()

    later = {}
    for h in range(heads):
        _, suffix = inside[h]
        high, low = split(suffix[:, :depth])
        state = carry_in[h]
        adjoint = dot(high, state) + dot(low, state) + suffix[:, depth:]
        for b in reversed(range(blocks)):
            later[h, b] = adjoint
            if b > 0:
                adjoint = mm(map_buf[h, b, :, :depth], adjoint) + map_buf[h, b, :, depth:]
    pairs = [(h, b) for h in range(heads) for b in range(blocks)]

    def by_parts(make):
        return jnp.concatenate([make(h, b) for h, b in pairs], axis=0)

    reads = [
        mm(jnp.concatenate([part(unit_k, h, b), part(unit_q, h, b)], axis=0), states_ref[b, h])
        for h, b in pairs
    ]
    key_reads = jnp.concatenate([item[:BLOCK] for item in reads], axis=0)
    query_reads = jnp.concatenate([item[BLOCK:] for item in reads], axis=0)
    remainder = values - growth * key_reads
    fresh = mm(solved, beta * remainder)
    fresh_grad = pulled + by_parts(lambda h, b: mm(part(tailing, h, b), later[h, b]))
    solved_grad = mm(solved, fresh_grad, TN)
    outer = mm(jnp.concatenate([out_grad, solved_grad], axis=0), fresh, NT)
    faded_grad = fading * outer[:total]
    lower_grad = -outer[total:]
    key_products_grad = beta * strict_fading * lower_grad
    value_grad = beta * solved_grad
    backs = [
        mm(
            jnp.concatenate([part(out_grad, h, b), part(value_grad, h, b)], axis=0),
            states_ref[b, h],
            NT,
        )
        for h, b in pairs
    ]
    out_back = jnp.concatenate([item[:BLOCK] for item in backs], axis=0)
    value_back = jnp.concatenate([item[BLOCK:] for item in backs], axis=0)
    fresh_back = tail * by_parts(lambda h, b: mm(part(fresh, h, b), later[h, b], NT))
    unit_q_grad = growth * out_back + mm(faded_grad, unit_k)
    unit_k_grad = (
        fresh_back
        - growth * value_back
        + mm(faded_grad, unit_q, TN)
        + mm(key_products_grad, unit_k)
        + mm(key_products_grad, unit_k, TN)
    )
    q_grad = scaling * inv_q * (unit_q_grad - raw_q * (inv_q * inv_q * row_sum(unit_q_grad * raw_q)))
    k_grad = inv_k * (unit_k_grad - raw_k * (inv_k * inv_k * row_sum(unit_k_grad * raw_k)))
    for h in range(heads):
        cols = slice(h * depth, (h + 1) * depth)
        own = slice(h * rows, (h + 1) * rows)
        gdq_out[:, cols] = q_grad[own].astype(BF16)
        gdk_out[:, cols] = k_grad[own].astype(BF16)
        gdv_out[:, cols] = value_grad[own].astype(BF16)
    beta_grad = row_sum(solved_grad * remainder) + row_sum(lower_grad * faded_keys)
    exponent = faded_grad * query_products + key_products_grad * key_products
    tail_grad = row_sum(unit_k * fresh_back)
    growth_grad = row_sum(out_grad * query_reads) - row_sum(value_grad * key_reads)
    summed_grad = (
        row_sum(exponent) - to_column(column_sum(exponent)) - tail_grad + growth * growth_grad
    )
    end_grad = end_growth * by_parts(
        lambda h, b: jnp.broadcast_to(
            column_sum(row_sum(later[h, b] * states_ref[b, h])), (BLOCK, 1)
        )
    )
    decay_grad = (
        column_sum(jnp.where(causal, summed_grad, 0.0))
        + column_sum(jnp.where(same, tail_grad, 0.0))
        + to_row(end_grad)
    )
    beta_row = to_row(beta_grad)
    for h in range(heads):
        own = slice(h * rows, (h + 1) * rows)
        gdecay_out[h : h + 1, :] = decay_grad[:, own]
        gbeta_out[h : h + 1, :] = beta_row[:, own]

    attend(1, last_reach)

    dq_out[...] = (dq_acc[...] * scaling).astype(BF16)
    both_grads = jnp.concatenate(
        [(dkv_acc[:, :columns] * scaling).astype(BF16), dkv_acc[:, columns:].astype(BF16)], axis=1
    )
    w_all[me] = w_ref[...]
    for j in range(1, n):
        w_copy(j).wait_recv()
    out_rows = dx_out.shape[0]
    pieces_each = out_rows // w_rows

    def dx_rows(owner):
        piece = w_all[pl.ds(owner * pieces_each, pieces_each)].reshape(out_rows, 2 * columns)
        return dot(piece, both_grads, NT)

    def dx_copy(j):
        return pltpu.make_async_remote_copy(
            src_ref=dx_send.at[j - 1],
            dst_ref=dx_recv.at[j - 1],
            send_sem=x_send.at[j - 1],
            recv_sem=x_recv.at[j - 1],
            device_id={"head": lax.rem(my_head + j, head_n)},
            device_id_type=MESH,
        )

    for j in range(1, head_n):
        dx_send[j - 1] = dx_rows(lax.rem(my_head + j, head_n))
        dx_copy(j).start()
    result = dx_rows(my_head)
    for j in range(1, head_n):
        dx_copy(j).wait_recv()
        result = result + dx_recv[j - 1]
    dx_out[...] = result.astype(BF16)

    for j in range(1, last_reach + 1):
        @pl.when(me + j < n)
        def _():
            kv_copy(j, 0).wait_send()
            kv_copy(j, 1).wait_send()

        @pl.when(me - j >= 0)
        def _():
            qd_copy(j, 0).wait_send()
            qd_copy(j, 1).wait_send()
            st_copy(j).wait_send()

    for j in range(1, n):
        w_copy(j).wait_send()
    for j in range(1, size):
        ab_copy(j).wait_send()
    if groups > 1:
        @pl.when(group > 0)
        def _():
            carry_copy().wait_send()

    for j in range(1, head_n):
        dx_copy(j).wait_send()


def per_device(n, head_n, *args):
    attn_q, attn_lse, w_kv, states = args[0], args[5], args[6], args[13]
    rows, columns = attn_q.shape
    heads = attn_lse.shape[0]
    depth = columns // heads
    reach = min(WINDOW // rows, n - 1)
    size = group_size(n)
    blocks = states.shape[0]
    w_rows = w_kv.shape[0]
    out_rows = n * w_rows // head_n
    args = list(args)
    args[6] = w_kv.reshape(w_rows, 2 * columns)
    dma = pltpu.SemaphoreType.DMA
    vmem = pl.BlockSpec(memory_space=pltpu.VMEM)
    others = max(head_n - 1, 1)
    return pl.pallas_call(
        functools.partial(kernel, n, head_n),
        out_shape=(
            jax.ShapeDtypeStruct((rows, columns), BF16),
            jax.ShapeDtypeStruct((out_rows, rows), BF16),
            jax.ShapeDtypeStruct((rows, columns), BF16),
            jax.ShapeDtypeStruct((rows, columns), BF16),
            jax.ShapeDtypeStruct((rows, columns), BF16),
            jax.ShapeDtypeStruct((heads, rows), F32),
            jax.ShapeDtypeStruct((heads, rows), F32),
        ),
        in_specs=[vmem] * len(args),
        out_specs=(vmem,) * 7,
        scratch_shapes=[
            pltpu.VMEM((reach, 2, rows, columns), BF16),
            pltpu.VMEM((reach, 2, rows, columns), BF16),
            pltpu.VMEM((2 * heads, rows), F32),
            pltpu.VMEM((reach, 2 * heads, rows), F32),
            pltpu.VMEM((n, w_rows, 2 * columns), BF16),
            pltpu.VMEM((size, heads, depth, 2 * depth), BF16),
            pltpu.VMEM((heads, depth, depth), BF16),
            pltpu.VMEM((heads, depth, depth), BF16),
            pltpu.VMEM((others, out_rows, rows), F32),
            pltpu.VMEM((others, out_rows, rows), F32),
            pltpu.VMEM((rows, columns), F32),
            pltpu.VMEM((rows, 2 * columns), F32),
            pltpu.VMEM((heads, blocks, depth, 2 * depth), F32),
            dma((reach, 2)), dma((reach, 2)),
            dma((reach, 2)), dma((reach, 2)),
            dma((reach,)), dma((reach,)),
            dma((n,)), dma((n,)),
            dma((size,)), dma((size,)),
            dma, dma,
            dma((others,)), dma((others,)),
        ],
        compiler_params=pltpu.CompilerParams(
            collective_id=0, has_side_effects=True, vmem_limit_bytes=60000000
        ),
        name="layer_backward",
    )(*args)


def solution(mesh):
    rows = P("seq", "head")
    gates = P("head", "seq")
    return jax.shard_map(
        functools.partial(per_device, mesh.shape["seq"], mesh.shape["head"]),
        mesh=mesh,
        in_specs=(
            rows, rows, rows, rows, rows, gates, P("seq", None, "head"),
            rows, rows, rows, rows, gates, gates, P("seq", "head", None, None),
        ),
        out_specs=(rows, gates, rows, rows, rows, gates, gates),
        check_vma=False,
    )
```

time: 313 us -> 77.6 us (0.25)
  waiting for transfers between devices: 112 us -> 0 us
  starting transfers between devices: 70.6 us -> 0 us
  Pallas kernels: 0 us -> 68.9 us
  blocking collectives: 54.2 us -> 0 us
  matrix products: 31.3 us -> 0 us
  between operations: 15.6 us -> 0.66 us
  local copies, waits for them, and re-layouts: 19.6 us -> 7.37 us
  other arithmetic: 7.44 us -> 0 us
    ppermute x39 -> x0, waiting for transfers between devices: 112 us -> none  [from_behind(): return lax.ppermute(block, axis, route)]
    ppermute x39 -> x0, starting transfers between devices: 70.6 us -> none  [from_behind(): return lax.ppermute(block, axis, route)]
    pallas_call x0 -> x1, Pallas kernels: none -> 68.9 us  [per_device(): pl.pallas_call(functools.partial(kernel, n, head_n), out_shape=(jax.Shape...]
    all_gather x1 -> x0, blocking collectives: 54.2 us -> none  [per_device(): row_piece = lax.all_gather(w_kv, 'seq', axis=0, tiled=True)]
    dot_general x81 -> x0, matrix products: 31.3 us -> none  [the longest x53 21.9 us: matmul(): return jnp.dot(left_side, right_side, precision=HIGH)]
    unnamed x98 -> x20, local copies, waits for them, and re-layouts: 11.8 us -> 7.37 us
    reshape x8 -> x0, local copies, waits for them, and re-layouts: 3.71 us -> none  [the longest x4 1.54 us: gates_by_blocks(): return matrix.reshape(head_count, block_count, BLOCK).transpose(1, 0, 2)]
  transfers between devices with their start and end apart: 40 -> 0, of which waited for: 17 -> 0; matrix products, arithmetic and copies ran while one was open for 16% -> 0% of each run, Pallas kernels for 0% -> 0%
where the time goes in v1:
time: 77.6 us; the launch traced here: 76.9 us
  Pallas kernels  68.9 us (89%)
  local copies, waits for them, and re-layouts  7.37 us (9%)
    pallas_call x1, Pallas kernels, per_device(): pl.pallas_call(functools.partial(kernel, n, head_n), out_shape=(jax.Shape...  68.9 us
    unnamed x20, local copies, waits for them, and re-layouts  7.37 us

profile of v1, /device:TPU:0, one launch (start us, length us, event | category | flops | bytes accessed | tf_op | source)
XLA Modules:
  0.0 76.9 jit_solution(4550661364643069080)
XLA Ops:
  0.6 1.4 %copy.21 = bf16[4,8,2,256]{3,1,2,0:T(8,128)(2,1)} copy(bf16[4,8,2,256]{3,2,1,0:T(2,128)(2,1)} %bitcast.3) | data formatting | bytes 65536
  2.0 68.9 %layer_backward.1 = (bf16[128,256]{1,0:T(8,128)(2,1)}, bf16[256,128]{1,0:T(8,128)(2,1)}, bf16[128,256]{1,0:T(8,128)(2,1)}, bf16[128,256]{1,0:T(8,128)(2,1)}, bf1...) custom-call(bf16[128,256]{1,0:T(8,128)(2,1)} %q_ref.1, bf16[128,256]{1,0:T(8,128)(2,1)} %k_ref.1, ...), custom_call_target="tpu_custom_call" | custom-call | tf_op jit(solution)/shard_map/layer_backward/pallas_call | solution.py:531
  70.9 0.0 copy-start.3
  70.9 1.5 %copy.29 = bf16[128,256]{1,0:T(8,128)(2,1)} copy(bf16[128,256]{1,0:T(8,128)(2,1)} %get-tuple-element.14) | data formatting | bytes 131072
  72.4 0.0 copy-done.3
  72.4 0.0 copy-start.2
  72.4 0.6 copy.30
  73.0 0.2 copy-done.2
  73.3 0.0 copy-start.1
  73.3 0.6 copy.31
  73.9 0.2 copy-done.1
  74.1 0.0 copy-start
  74.1 0.6 copy.32
  74.8 0.2 copy-done
  75.0 0.0 copy-start.5
  75.0 0.6 copy.33
  75.6 0.0 copy-done.5
  75.7 0.0 copy-start.4
  75.7 0.6 copy.34
  76.2 0.1 copy-done.4
  76.3 0.6 copy.35
Async XLA Ops:
  70.9 1.5 %copy-start.3 = (bf16[256,128]{1,0:T(8,128)(2,1)S(1)}, bf16[256,128]{1,0:T(8,128)(2,1)}, u32[]{:S(2)}) copy-start(bf16[256,128]{1,0:T(8,128)(2,1)} %get-tuple-element.15) | copy-start | bytes 196612
  72.4 0.9 %copy-start.2 = (bf16[128,256]{1,0:T(8,128)(2,1)S(1)}, bf16[128,256]{1,0:T(8,128)(2,1)}, u32[]{:S(2)}) copy-start(bf16[128,256]{1,0:T(8,128)(2,1)} %get-tuple-element.16) | copy-start | bytes 196612
  73.3 0.9 %copy-start.1 = (bf16[128,256]{1,0:T(8,128)(2,1)S(1)}, bf16[128,256]{1,0:T(8,128)(2,1)}, u32[]{:S(2)}) copy-start(bf16[128,256]{1,0:T(8,128)(2,1)} %get-tuple-element.17) | copy-start | bytes 196612
  74.1 0.9 %copy-start = (bf16[128,256]{1,0:T(8,128)(2,1)S(1)}, bf16[128,256]{1,0:T(8,128)(2,1)}, u32[]{:S(2)}) copy-start(bf16[128,256]{1,0:T(8,128)(2,1)} %get-tuple-element.18) | copy-start | bytes 196612
  75.0 0.7 copy-start.5
  75.7 0.7 copy-start.4

commit v2 on v1

--- a/solution.py
+++ b/solution.py
@@ -54,11 +54,13 @@
     return jnp.concatenate([matrix[:, h * depth : (h + 1) * depth] for h in range(heads)], axis=0)
 
 
-def group_size(count):
+def group_size(count, reach):
     size = 1
     while size * size < count:
         size *= 2
-    return size if count % size == 0 else count
+    while count % size or reach % size:
+        size //= 2
+    return size
 
 
 def kernel(
@@ -70,6 +72,7 @@
     kv_buf, qd_buf, stat_own, stat_buf, w_all, ab_buf, carry_in, carry_out, dx_send, dx_recv,
     dq_acc, dkv_acc, map_buf,
     kv_send, kv_recv, qd_send, qd_recv, st_send, st_recv, w_send, w_recv,
+    kv_pass, qd_pass, st_pass, w_pass,
     ab_send, ab_recv, c_send, c_recv, x_send, x_recv,
 ):
     me = lax.axis_index("seq")
@@ -80,7 +83,7 @@
     reach = WINDOW // rows
     blocks = rows // BLOCK
     total = heads * rows
-    size = group_size(n)
+    size = group_size(n, WINDOW // rows)
     groups = n // size
     rank = lax.rem(me, size)
     group = lax.div(me, size)
@@ -104,47 +107,132 @@
         stat_own[heads + h : heads + h + 1, :] = mm_full(ones, product, NT)[0:1, :]
     pl.semaphore_wait(barrier, n - 1 + head_n - 1)
 
-    def kv_copy(j, which):
+    hops = min(reach // size, groups - 1)
+
+    def move(source, target, sent, received, index):
         return pltpu.make_async_remote_copy(
-            src_ref=(k_ref, v_ref)[which],
-            dst_ref=kv_buf.at[j - 1, which],
-            send_sem=kv_send.at[j - 1, which],
-            recv_sem=kv_recv.at[j - 1, which],
-            device_id={"seq": lax.rem(me + j, n)},
+            src_ref=source,
+            dst_ref=target,
+            send_sem=sent,
+            recv_sem=received,
+            device_id={"seq": index},
             device_id_type=MESH,
         )
 
-    def qd_copy(j, which):
-        return pltpu.make_async_remote_copy(
-            src_ref=(q_ref, dout_ref)[which],
-            dst_ref=qd_buf.at[j - 1, which],
-            send_sem=qd_send.at[j - 1, which],
-            recv_sem=qd_recv.at[j - 1, which],
-            device_id={"seq": lax.rem(me + n - j, n)},
-            device_id_type=MESH,
-        )
-
-    def st_copy(j):
-        return pltpu.make_async_remote_copy(
-            src_ref=stat_own,
-            dst_ref=stat_buf.at[j - 1],
-            send_sem=st_send.at[j - 1],
-            recv_sem=st_recv.at[j - 1],
-            device_id={"seq": lax.rem(me + n - j, n)},
-            device_id_type=MESH,
-        )
+    def kv_copies(j):
+        index = lax.rem(me + j, n)
+        return [
+            move(
+                (k_ref, v_ref)[i], kv_buf.at[j - 1, i],
+                kv_send.at[j - 1, i], kv_recv.at[j - 1, i], index,
+            )
+            for i in range(2)
+        ]
+
+    def qd_copies(j):
+        index = lax.rem(me + n - j, n)
+        return [
+            move(
+                (q_ref, dout_ref)[i], qd_buf.at[j - 1, i],
+                qd_send.at[j - 1, i], qd_recv.at[j - 1, i], index,
+            )
+            for i in range(2)
+        ] + [move(stat_own, stat_buf.at[j - 1], st_send.at[j - 1], st_recv.at[j - 1], index)]
+
+    def kv_passes(m, i):
+        peer = lax.rem(rank + i, size)
+        slot = m * size + peer - rank - 1
+        return [
+            move(
+                kv_buf.at[m * size - 1, c], kv_buf.at[slot, c],
+                kv_pass.at[m - 1, i, c], kv_recv.at[slot, c], first + peer,
+            )
+            for c in range(2)
+        ]
+
+    def qd_passes(m, i):
+        peer = lax.rem(rank + i, size)
+        slot = m * size + rank - peer - 1
+        return [
+            move(
+                qd_buf.at[m * size - 1, c], qd_buf.at[slot, c],
+                qd_pass.at[m - 1, i, c], qd_recv.at[slot, c], first + peer,
+            )
+            for c in range(2)
+        ] + [
+            move(
+                stat_buf.at[m * size - 1], stat_buf.at[slot],
+                st_pass.at[m - 1, i], st_recv.at[slot], first + peer,
+            )
+        ]
+
+    def kv_goes(m, i):
+        peer = lax.rem(rank + i, size)
+        return (group >= m) & (m * size + peer - rank <= reach)
+
+    def qd_goes(m, i):
+        peer = lax.rem(rank + i, size)
+        return (group + m < groups) & (m * size + rank - peer <= reach)
 
     w_rows = w_ref.shape[0]
 
-    def w_copy(j):
-        return pltpu.make_async_remote_copy(
-            src_ref=w_ref,
-            dst_ref=w_all.at[me],
-            send_sem=w_send.at[j - 1],
-            recv_sem=w_recv.at[j - 1],
-            device_id={"seq": lax.rem(me + j, n)},
-            device_id_type=MESH,
-        )
+    def w_copy(m):
+        return move(
+            w_ref, w_all.at[me], w_send.at[m - 1], w_recv.at[0, m], lax.rem(me + m * size, n)
+        )
+
+    def w_passes(i):
+        peer = lax.rem(rank + i, size)
+        return [
+            move(
+                w_ref if m == 0 else w_all.at[lax.rem(me + n - m * size, n)],
+                w_all.at[lax.rem(me + n - m * size, n)],
+                w_pass.at[i, m], w_recv.at[i, m], first + peer,
+            )
+            for m in range(groups)
+        ]
+
+    def each(copies, act):
+        for copy in copies:
+            getattr(copy, act)()
+
+    def own_copies(act):
+        for m in range(1, hops + 1):
+            @pl.when(group + m < groups)
+            def _():
+                each(kv_copies(m * size), act)
+
+            @pl.when(group >= m)
+            def _():
+                each(qd_copies(m * size), act)
+
+        for j in range(1, size):
+            @pl.when(rank + j < size)
+            def _():
+                each(kv_copies(j), act)
+
+            @pl.when(rank >= j)
+            def _():
+                each(qd_copies(j), act)
+
+    def pass_copies(m, act):
+        for i in range(1, size):
+            @pl.when(kv_goes(m, i))
+            def _():
+                each(kv_passes(m, i), act)
+
+            @pl.when(qd_goes(m, i))
+            def _():
+                each(qd_passes(m, i), act)
+
+    def take_column(m):
+        @pl.when(group >= m)
+        def _():
+            each(kv_copies(m * size), "wait_recv")
+
+        @pl.when(group + m < groups)
+        def _():
+            each(qd_copies(m * size), "wait_recv")
 
     def ab_copy(j):
         return pltpu.make_async_remote_copy(
@@ -166,23 +254,9 @@
             device_id_type=MESH,
         )
 
-    last_reach = min(reach, n - 1)
-    near = min(size, last_reach)
-
-    def start_offsets(low, high):
-        for j in range(low, high + 1):
-            @pl.when(me + j < n)
-            def _():
-                kv_copy(j, 0).start()
-                kv_copy(j, 1).start()
-
-            @pl.when(me - j >= 0)
-            def _():
-                qd_copy(j, 0).start()
-                qd_copy(j, 1).start()
-                st_copy(j).start()
-
-    start_offsets(1, near)
+    own_copies("start")
+    for m in range(1, groups):
+        w_copy(m).start()
 
     row_ids = lax.broadcasted_iota(jnp.int32, (total, total), 0)
     col_ids = lax.broadcasted_iota(jnp.int32, (total, total), 1)
@@ -297,18 +371,22 @@
 
     for j in range(1, size):
         ab_copy(j).start()
-    start_offsets(near + 1, last_reach)
-    for j in range(1, n):
-        w_copy(j).start()
-
-    def attend(low, high):
-        for j in range(low, high + 1):
+    for m in range(1, hops + 1):
+        take_column(m)
+        pass_copies(m, "start")
+    for m in range(1, groups):
+        w_copy(m).wait_recv()
+    for i in range(1, size):
+        each(w_passes(i), "start")
+
+    def attend(distances, keys_here, queries_here):
+        for j in distances:
             mask = query_ids + j * rows - key_ids < WINDOW if (j + 1) * rows > WINDOW else None
 
-            @pl.when(me - j >= 0)
-            def _():
-                kv_copy(j, 0).wait_recv()
-                kv_copy(j, 1).wait_recv()
+            @pl.when(keys_here(j))
+            def _():
+                if j % size:
+                    each(kv_copies(j), "wait_recv")
                 for h in range(heads):
                     cols = slice(h * depth, (h + 1) * depth)
                     keys = kv_buf[j - 1, 0, :, cols]
@@ -318,11 +396,10 @@
                     )
                     dq_acc[:, cols] += dot(grad_logit, keys, TN)
 
-            @pl.when(me + j < n)
-            def _():
-                qd_copy(j, 0).wait_recv()
-                qd_copy(j, 1).wait_recv()
-                st_copy(j).wait_recv()
+            @pl.when(queries_here(j))
+            def _():
+                if j % size:
+                    each(qd_copies(j), "wait_recv")
                 for h in range(heads):
                     cols = slice(h * depth, (h + 1) * depth)
                     queries = qd_buf[j - 1, 0, :, cols]
@@ -337,6 +414,29 @@
                         weights, grads
                     )
 
+    attend(range(1, size), lambda j: rank >= j, lambda j: rank + j < size)
+    attend(
+        range(size, hops * size + 1, size), lambda j: me >= j, lambda j: me + j < n
+    )
+
+    pairs = [(h, b) for h in range(heads) for b in range(blocks)]
+
+    def by_parts(make):
+        return jnp.concatenate([make(h, b) for h, b in pairs], axis=0)
+
+    reads = [
+        mm(jnp.concatenate([part(unit_k, h, b), part(unit_q, h, b)], axis=0), states_ref[b, h])
+        for h, b in pairs
+    ]
+    key_reads = jnp.concatenate([item[:BLOCK] for item in reads], axis=0)
+    query_reads = jnp.concatenate([item[BLOCK:] for item in reads], axis=0)
+    remainder = values - growth * key_reads
+    fresh = mm(solved, beta * remainder)
+    faded_grad = fading * mm(out_grad, fresh, NT)
+    out_back = by_parts(lambda h, b: mm(part(out_grad, h, b), states_ref[b, h], NT))
+    unit_q_grad = growth * out_back + mm(faded_grad, unit_k)
+    faded_back = mm(faded_grad, unit_q, TN)
+
     for j in range(1, size):
         ab_copy(j).wait_recv()
     inside = []
@@ -383,42 +483,17 @@
             later[h, b] = adjoint
             if b > 0:
                 adjoint = mm(map_buf[h, b, :, :depth], adjoint) + map_buf[h, b, :, depth:]
-    pairs = [(h, b) for h in range(heads) for b in range(blocks)]
-
-    def by_parts(make):
-        return jnp.concatenate([make(h, b) for h, b in pairs], axis=0)
-
-    reads = [
-        mm(jnp.concatenate([part(unit_k, h, b), part(unit_q, h, b)], axis=0), states_ref[b, h])
-        for h, b in pairs
-    ]
-    key_reads = jnp.concatenate([item[:BLOCK] for item in reads], axis=0)
-    query_reads = jnp.concatenate([item[BLOCK:] for item in reads], axis=0)
-    remainder = values - growth * key_reads
-    fresh = mm(solved, beta * remainder)
     fresh_grad = pulled + by_parts(lambda h, b: mm(part(tailing, h, b), later[h, b]))
     solved_grad = mm(solved, fresh_grad, TN)
-    outer = mm(jnp.concatenate([out_grad, solved_grad], axis=0), fresh, NT)
-    faded_grad = fading * outer[:total]
-    lower_grad = -outer[total:]
+    lower_grad = -mm(solved_grad, fresh, NT)
     key_products_grad = beta * strict_fading * lower_grad
     value_grad = beta * solved_grad
-    backs = [
-        mm(
-            jnp.concatenate([part(out_grad, h, b), part(value_grad, h, b)], axis=0),
-            states_ref[b, h],
-            NT,
-        )
-        for h, b in pairs
-    ]
-    out_back = jnp.concatenate([item[:BLOCK] for item in backs], axis=0)
-    value_back = jnp.concatenate([item[BLOCK:] for item in backs], axis=0)
+    value_back = by_parts(lambda h, b: mm(part(value_grad, h, b), states_ref[b, h], NT))
     fresh_back = tail * by_parts(lambda h, b: mm(part(fresh, h, b), later[h, b], NT))
-    unit_q_grad = growth * out_back + mm(faded_grad, unit_k)
     unit_k_grad = (
         fresh_back
         - growth * value_back
-        + mm(faded_grad, unit_q, TN)
+        + faded_back
         + mm(key_products_grad, unit_k)
         + mm(key_products_grad, unit_k, TN)
     )
@@ -453,15 +528,19 @@
         gdecay_out[h : h + 1, :] = decay_grad[:, own]
         gbeta_out[h : h + 1, :] = beta_row[:, own]
 
-    attend(1, last_reach)
+    attend(
+        [j for j in range(1, min(reach, n - 1) + 1) if j % size],
+        lambda j: (me >= j) & (rank < j),
+        lambda j: (me + j < n) & (rank + j >= size),
+    )
 
     dq_out[...] = (dq_acc[...] * scaling).astype(BF16)
     both_grads = jnp.concatenate(
         [(dkv_acc[:, :columns] * scaling).astype(BF16), dkv_acc[:, columns:].astype(BF16)], axis=1
     )
     w_all[me] = w_ref[...]
-    for j in range(1, n):
-        w_copy(j).wait_recv()
+    for i in range(1, size):
+        each(w_passes(i), "wait_recv")
     out_rows = dx_out.shape[0]
     pieces_each = out_rows // w_rows
 
@@ -488,20 +567,13 @@
         result = result + dx_recv[j - 1]
     dx_out[...] = result.astype(BF16)
 
-    for j in range(1, last_reach + 1):
-        @pl.when(me + j < n)
-        def _():
-            kv_copy(j, 0).wait_send()
-            kv_copy(j, 1).wait_send()
-
-        @pl.when(me - j >= 0)
-        def _():
-            qd_copy(j, 0).wait_send()
-            qd_copy(j, 1).wait_send()
-            st_copy(j).wait_send()
-
-    for j in range(1, n):
-        w_copy(j).wait_send()
+    own_copies("wait_send")
+    for m in range(1, hops + 1):
+        pass_copies(m, "wait_send")
+    for m in range(1, groups):
+        w_copy(m).wait_send()
+    for i in range(1, size):
+        each(w_passes(i), "wait_send")
     for j in range(1, size):
         ab_copy(j).wait_send()
     if groups > 1:
@@ -513,14 +585,22 @@
         dx_copy(j).wait_send()
 
 
+def hand_over(*refs):
+    half = len(refs) // 2
+    for source, target in zip(refs[:half], refs[half:]):
+        target[...] = source[...]
+
+
 def per_device(n, head_n, *args):
     attn_q, attn_lse, w_kv, states = args[0], args[5], args[6], args[13]
     rows, columns = attn_q.shape
     heads = attn_lse.shape[0]
     depth = columns // heads
     reach = min(WINDOW // rows, n - 1)
-    size = group_size(n)
+    size = group_size(n, WINDOW // rows)
     blocks = states.shape[0]
+    groups = n // size
+    hops = max(min(reach // size, groups - 1), 1)
     w_rows = w_kv.shape[0]
     out_rows = n * w_rows // head_n
     args = list(args)
@@ -528,7 +608,7 @@
     dma = pltpu.SemaphoreType.DMA
     vmem = pl.BlockSpec(memory_space=pltpu.VMEM)
     others = max(head_n - 1, 1)
-    return pl.pallas_call(
+    results = pl.pallas_call(
         functools.partial(kernel, n, head_n),
         out_shape=(
             jax.ShapeDtypeStruct((rows, columns), BF16),
@@ -558,7 +638,8 @@
             dma((reach, 2)), dma((reach, 2)),
             dma((reach, 2)), dma((reach, 2)),
             dma((reach,)), dma((reach,)),
-            dma((n,)), dma((n,)),
+            dma((groups,)), dma((size, groups)),
+            dma((hops, size, 2)), dma((hops, size, 2)), dma((hops, size)), dma((size, groups)),
             dma((size,)), dma((size,)),
             dma, dma,
             dma((others,)), dma((others,)),
@@ -568,6 +649,13 @@
         ),
         name="layer_backward",
     )(*args)
+    return pl.pallas_call(
+        hand_over,
+        out_shape=[jax.ShapeDtypeStruct(item.shape, item.dtype) for item in results],
+        in_specs=[vmem] * len(results),
+        out_specs=[vmem] * len(results),
+        name="hand_over",
+    )(*results)
 
 
 def solution(mesh):

time: 77.6 us -> 50.3 us (0.65)
  the two profiles are of different devices: /device:TPU:0 before, /device:TPU:15 now
where the time goes in v2:
time: 50.3 us; the launch traced here: 50 us
  Pallas kernels  48 us (95%)
  local copies, waits for them, and re-layouts  1.38 us (3%)
  between operations  0.64 us (1%)
    pallas_call x1, Pallas kernels, per_device(): pl.pallas_call(functools.partial(kernel, n, head_n), out_shape=(jax.Shape...  46.3 us
    pallas_call x1, Pallas kernels, per_device(): pl.pallas_call(hand_over, out_shape=[jax.ShapeDtypeStruct(item.shape, ite...  1.7 us
    unnamed x1, local copies, waits for them, and re-layouts  1.38 us

profile of v2, /device:TPU:15, one launch (start us, length us, event | category | flops | bytes accessed | tf_op | source)
XLA Modules:
  0.0 50.0 jit_solution(6315655577758876564)
XLA Ops:
  0.6 1.4 %copy.21 = bf16[4,8,2,256]{3,1,2,0:T(8,128)(2,1)} copy(bf16[4,8,2,256]{3,2,1,0:T(2,128)(2,1)} %bitcast.3) | data formatting | bytes 65536
  2.0 46.3 %layer_backward.1 = (bf16[128,256]{1,0:T(8,128)(2,1)}, bf16[256,128]{1,0:T(8,128)(2,1)}, bf16[128,256]{1,0:T(8,128)(2,1)}, bf16[128,256]{1,0:T(8,128)(2,1)}, bf1...) custom-call(bf16[128,256]{1,0:T(8,128)(2,1)} %q_ref.1, bf16[128,256]{1,0:T(8,128)(2,1)} %k_ref.1, ...), custom_call_target="tpu_custom_call" | custom-call | tf_op jit(solution)/shard_map/layer_backward/pallas_call | solution.py:611
  48.3 1.7 %hand_over.1 = (bf16[128,256]{1,0:T(8,128)(2,1)}, bf16[256,128]{1,0:T(8,128)(2,1)}, bf16[128,256]{1,0:T(8,128)(2,1)}, bf16[128,256]{1,0:T(8,128)(2,1)}, bf16[128...) custom-call(bf16[128,256]{1,0:T(8,128)(2,1)} %get-tuple-element.14.refs_0_, ...), custom_call_target="tpu_custom_call" | custom-call | tf_op jit(solution)/shard_map/hand_over/pallas_call | solution.py:652

commit v3 on v2

--- a/solution.py
+++ b/solution.py
@@ -33,6 +33,10 @@
     return dot(left_high, right_high, dims) + (
         dot(left_high, right_low, dims) + dot(left_low, right_high, dims)
     )
+
+
+def mm_once(left, right, dims=NN):
+    return dot(left.astype(BF16), right.astype(BF16), dims)
 
 
 def mm_full(left, right, dims=NN):
@@ -215,21 +219,24 @@
             def _():
                 each(qd_copies(j), act)
 
-    def pass_copies(m, act):
+    def pass_keys(m, act):
         for i in range(1, size):
             @pl.when(kv_goes(m, i))
             def _():
                 each(kv_passes(m, i), act)
 
+    def pass_queries(m, act):
+        for i in range(1, size):
             @pl.when(qd_goes(m, i))
             def _():
                 each(qd_passes(m, i), act)
 
-    def take_column(m):
+    def take_keys(m):
         @pl.when(group >= m)
         def _():
             each(kv_copies(m * size), "wait_recv")
 
+    def take_queries(m):
         @pl.when(group + m < groups)
         def _():
             each(qd_copies(m * size), "wait_recv")
@@ -301,14 +308,17 @@
     faded_keys = strict_fading * key_products
     lower = beta * faded_keys
     solved = jnp.where(eye, 1.0, 0.0) - lower
-    powered = mm_full(lower, lower)
+    powered = mm(lower, lower)
     for step in range(BLOCK.bit_length() - 2):
         if step < BLOCK.bit_length() - 3:
-            both = mm_full(jnp.concatenate([solved, powered], axis=0), powered)
+            both = mm(jnp.concatenate([solved, powered], axis=0), powered)
             solved = solved + both[:total]
             powered = both[total:]
         else:
-            solved = solved + mm_full(solved, powered)
+            solved = solved + mm(solved, powered)
+    if hops:
+        take_keys(1)
+        pass_keys(1, "start")
     attention = fading * query_products
     widened = mm(solved, (beta * growth) * unit_k)
     pulled = mm(attention, out_grad, TN)
@@ -372,8 +382,11 @@
     for j in range(1, size):
         ab_copy(j).start()
     for m in range(1, hops + 1):
-        take_column(m)
-        pass_copies(m, "start")
+        if m > 1:
+            take_keys(m)
+            pass_keys(m, "start")
+        take_queries(m)
+        pass_queries(m, "start")
     for m in range(1, groups):
         w_copy(m).wait_recv()
     for i in range(1, size):
@@ -433,9 +446,9 @@
     remainder = values - growth * key_reads
     fresh = mm(solved, beta * remainder)
     faded_grad = fading * mm(out_grad, fresh, NT)
-    out_back = by_parts(lambda h, b: mm(part(out_grad, h, b), states_ref[b, h], NT))
-    unit_q_grad = growth * out_back + mm(faded_grad, unit_k)
-    faded_back = mm(faded_grad, unit_q, TN)
+    out_back = by_parts(lambda h, b: mm_once(part(out_grad, h, b), states_ref[b, h], NT))
+    unit_q_grad = growth * out_back + mm_once(faded_grad, unit_k)
+    faded_back = mm_once(faded_grad, unit_q, TN)
 
     for j in range(1, size):
         ab_copy(j).wait_recv()
@@ -488,14 +501,14 @@
     lower_grad = -mm(solved_grad, fresh, NT)
     key_products_grad = beta * strict_fading * lower_grad
     value_grad = beta * solved_grad
-    value_back = by_parts(lambda h, b: mm(part(value_grad, h, b), states_ref[b, h], NT))
+    value_back = by_parts(lambda h, b: mm_once(part(value_grad, h, b), states_ref[b, h], NT))
     fresh_back = tail * by_parts(lambda h, b: mm(part(fresh, h, b), later[h, b], NT))
     unit_k_grad = (
         fresh_back
         - growth * value_back
         + faded_back
-        + mm(key_products_grad, unit_k)
-        + mm(key_products_grad, unit_k, TN)
+        + mm_once(key_products_grad, unit_k)
+        + mm_once(key_products_grad, unit_k, TN)
     )
     q_grad = scaling * inv_q * (unit_q_grad - raw_q * (inv_q * inv_q * row_sum(unit_q_grad * raw_q)))
     k_grad = inv_k * (unit_k_grad - raw_k * (inv_k * inv_k * row_sum(unit_k_grad * raw_k)))
@@ -569,7 +582,8 @@
 
     own_copies("wait_send")
     for m in range(1, hops + 1):
-        pass_copies(m, "wait_send")
+        pass_keys(m, "wait_send")
+        pass_queries(m, "wait_send")
     for m in range(1, groups):
         w_copy(m).wait_send()
     for i in range(1, size):

time: 50.3 us -> 50.1 us (level)
  the two profiles are of different devices: /device:TPU:15 before, /device:TPU:3 now
where the time goes in v3:
time: 50.1 us; the launch traced here: 49.8 us
  Pallas kernels  47.8 us (95%)
  local copies, waits for them, and re-layouts  1.38 us (3%)
  between operations  0.64 us (1%)
    pallas_call x1, Pallas kernels, per_device(): pl.pallas_call(functools.partial(kernel, n, head_n), out_shape=(jax.Shape...  46.1 us
    pallas_call x1, Pallas kernels, per_device(): pl.pallas_call(hand_over, out_shape=[jax.ShapeDtypeStruct(item.shape, ite...  1.7 us
    unnamed x1, local copies, waits for them, and re-layouts  1.38 us

profile of v3, /device:TPU:3, one launch (start us, length us, event | category | flops | bytes accessed | tf_op | source)
XLA Modules:
  0.0 49.8 jit_solution(6653607230045454929)
XLA Ops:
  0.6 1.4 %copy.21 = bf16[4,8,2,256]{3,1,2,0:T(8,128)(2,1)} copy(bf16[4,8,2,256]{3,2,1,0:T(2,128)(2,1)} %bitcast.3) | data formatting | bytes 65536
  2.0 46.1 %layer_backward.1 = (bf16[128,256]{1,0:T(8,128)(2,1)}, bf16[256,128]{1,0:T(8,128)(2,1)}, bf16[128,256]{1,0:T(8,128)(2,1)}, bf16[128,256]{1,0:T(8,128)(2,1)}, bf1...) custom-call(bf16[128,256]{1,0:T(8,128)(2,1)} %q_ref.1, bf16[128,256]{1,0:T(8,128)(2,1)} %k_ref.1, ...), custom_call_target="tpu_custom_call" | custom-call | tf_op jit(solution)/shard_map/layer_backward/pallas_call | solution.py:625
  48.1 1.7 %hand_over.1 = (bf16[128,256]{1,0:T(8,128)(2,1)}, bf16[256,128]{1,0:T(8,128)(2,1)}, bf16[128,256]{1,0:T(8,128)(2,1)}, bf16[128,256]{1,0:T(8,128)(2,1)}, bf16[128...) custom-call(bf16[128,256]{1,0:T(8,128)(2,1)} %get-tuple-element.14.refs_0_, ...), custom_call_target="tpu_custom_call" | custom-call | tf_op jit(solution)/shard_map/hand_over/pallas_call | solution.py:666

commit v4 on v3

--- a/solution.py
+++ b/solution.py
@@ -316,9 +316,14 @@
             powered = both[total:]
         else:
             solved = solved + mm(solved, powered)
+    early = group < groups - 2
+
     if hops:
-        take_keys(1)
-        pass_keys(1, "start")
+        @pl.when(early)
+        def _():
+            take_keys(1)
+            pass_keys(1, "start")
+
     attention = fading * query_products
     widened = mm(solved, (beta * growth) * unit_k)
     pulled = mm(attention, out_grad, TN)
@@ -385,6 +390,12 @@
         if m > 1:
             take_keys(m)
             pass_keys(m, "start")
+        else:
+            @pl.when(jnp.logical_not(early))
+            def _():
+                take_keys(1)
+                pass_keys(1, "start")
+
         take_queries(m)
         pass_queries(m, "start")
     for m in range(1, groups):

time: 50.1 us -> 49 us (0.978)
  the two profiles are of different devices: /device:TPU:3 before, /device:TPU:13 now
where the time goes in v4:
time: 49 us; the launch traced here: 48.7 us
  Pallas kernels  46.7 us (95%)
  local copies, waits for them, and re-layouts  1.38 us (3%)
  between operations  0.64 us (1%)
    pallas_call x1, Pallas kernels, per_device(): pl.pallas_call(functools.partial(kernel, n, head_n), out_shape=(jax.Shape...  45 us
    pallas_call x1, Pallas kernels, per_device(): pl.pallas_call(hand_over, out_shape=[jax.ShapeDtypeStruct(item.shape, ite...  1.7 us
    unnamed x1, local copies, waits for them, and re-layouts  1.38 us

profile of v4, /device:TPU:13, one launch (start us, length us, event | category | flops | bytes accessed | tf_op | source)
XLA Modules:
  0.0 48.7 jit_solution(16634816006735587728)
XLA Ops:
  0.6 1.4 %copy.21 = bf16[4,8,2,256]{3,1,2,0:T(8,128)(2,1)} copy(bf16[4,8,2,256]{3,2,1,0:T(2,128)(2,1)} %bitcast.3) | data formatting | bytes 65536
  2.0 45.0 %layer_backward.1 = (bf16[128,256]{1,0:T(8,128)(2,1)}, bf16[256,128]{1,0:T(8,128)(2,1)}, bf16[128,256]{1,0:T(8,128)(2,1)}, bf16[128,256]{1,0:T(8,128)(2,1)}, bf1...) custom-call(bf16[128,256]{1,0:T(8,128)(2,1)} %q_ref.1, bf16[128,256]{1,0:T(8,128)(2,1)} %k_ref.1, ...), custom_call_target="tpu_custom_call" | custom-call | tf_op jit(solution)/shard_map/layer_backward/pallas_call | solution.py:636
  47.0 1.7 %hand_over.1 = (bf16[128,256]{1,0:T(8,128)(2,1)}, bf16[256,128]{1,0:T(8,128)(2,1)}, bf16[128,256]{1,0:T(8,128)(2,1)}, bf16[128,256]{1,0:T(8,128)(2,1)}, bf16[128...) custom-call(bf16[128,256]{1,0:T(8,128)(2,1)} %get-tuple-element.14.refs_0_, ...), custom_call_target="tpu_custom_call" | custom-call | tf_op jit(solution)/shard_map/hand_over/pallas_call | solution.py:677
